TPU v7x, 128 devices: a whole 4x4x4 slice. The times are simulated.
128 devices in a mesh: brick: 32 (over x, z_lo, y), scan: 4 (over z_hi, core).
Axes of the slice: x: 4, y: 4, z: 4 (z_hi: 2, z_lo: 2; z = z_hi * 2 + z_lo), core: 2. Of those that a mesh axis runs over, the one named last changes fastest.
Arguments:
- tomogram: bfloat16 [1024, 128, 128], P(('brick', 'scan')), may hold values from -6 to 6
- deformed: bfloat16 [4, 1024, 128, 128], P('scan', 'brick'), may hold values from -6 to 6
- subvoxel: float32 [4, 3, 32, 25], P('scan', None, 'brick'), may hold values from 0 to 0.99
- offsets: int32 [4, 3, 512], P('scan', None, 'brick'), may hold values from -15 to 15, as said below
Outputs:
- residual_map: bfloat16 [4, 1024, 128, 128], P('scan', 'brick')
- node_rhs: float32 [4, 3, 32, 25], P('scan', None, 'brick')
Inputs may be any that keep to these rules, and one draw needn't show every extreme that they name: offsets[k, c, e] lies in -(15) .. 15 and both ends occur.
All inputs are finite; a program needn't handle non-finite values.
Results may differ from a plain program's by a relative error of at most 0.0095.
Values may be sent and summed in bfloat16 or wider, within the bound.
A program may use at most 128 MiB of HBM per device.

v0:
```python
import jax
import jax.numpy as jnp
from jax import lax
from jax.sharding import PartitionSpec as P

E = 32
HALO = 16
RADIUS = 3


gauss_sigma = 1.0


def padded_2(cells, sides, width):
    for axis, dim in sides:
        count = lax.axis_size(axis)
        ends = count - 1
        head = lax.slice_in_dim(cells, 0, width, axis=dim)
        tail = lax.slice_in_dim(cells, cells.shape[dim] - width, cells.shape[dim], axis=dim)
        cells = jnp.concatenate(
            [
                lax.ppermute(tail, axis, [(i, (i + 1) % count) for i in range(ends)]),
                cells,
                lax.ppermute(head, axis, [((i + 1) % count, i) for i in range(ends)]),
            ],
            axis=dim,
        )
    return cells


def passed_along(block, axis, distance):
    devices = range(lax.axis_size(axis))
    route = [(i - distance, i) for i in devices if i - distance in devices]
    return lax.ppermute(block, axis, route)


def filter_taps():
    tap_pos = jnp.arange(-RADIUS, RADIUS + 1).astype(jnp.float32)
    gaussian = jnp.exp(-tap_pos * tap_pos / (2.0 * gauss_sigma * gauss_sigma))
    smooth_taps = gaussian / jnp.sum(gaussian)
    slope_taps = tap_pos * gaussian / jnp.sum(tap_pos * tap_pos * gaussian)
    return (smooth_taps.astype(jnp.bfloat16), slope_taps.astype(jnp.bfloat16))


def band_matrix(coeff, cross_width):
    distance = jnp.arange(cross_width)[:, None] - jnp.arange(cross_width)[None, :]
    band_table = jnp.zeros((cross_width, cross_width), jnp.float32)
    for tap in range(2 * RADIUS + 1):
        band_table = band_table + jnp.where(
            distance == tap - RADIUS, coeff[tap].astype(jnp.float32), jnp.float32(0.0)
        )
    return band_table.astype(jnp.bfloat16)


def z_stencil(field, coeff, planes):
    stencil_sum = jnp.zeros((planes,) + field.shape[1:], jnp.float32)
    for tap in range(2 * RADIUS + 1):
        stencil_sum = stencil_sum + coeff[tap].astype(jnp.float32) * field[
            tap : tap + planes
        ].astype(jnp.float32)
    return stencil_sum.astype(jnp.bfloat16)


def gradients(extended):
    smooth_taps, slope_taps = filter_taps()
    cross_width = extended.shape[2]
    planes = extended.shape[0] - 2 * RADIUS
    along_s = band_matrix(smooth_taps, cross_width)
    along_d = band_matrix(slope_taps, cross_width)
    both_bands = jnp.concatenate([along_s, along_d], axis=1)
    x_filtered = jnp.dot(
        extended.reshape(-1, cross_width), both_bands, preferred_element_type=jnp.float32
    )
    x_filtered = x_filtered.astype(jnp.bfloat16).reshape(
        extended.shape[0], extended.shape[1], 2 * cross_width
    )
    y_smoothed = jnp.einsum(
        "zyx,yw->zwx", x_filtered, along_s, preferred_element_type=jnp.float32
    ).astype(jnp.bfloat16)
    y_slope = jnp.einsum(
        "zyx,yw->zwx", x_filtered[:, :, :cross_width], along_d, preferred_element_type=jnp.float32
    ).astype(jnp.bfloat16)
    grad_z = z_stencil(y_smoothed[:, :, :cross_width], slope_taps, planes)
    grad_y = z_stencil(y_slope, smooth_taps, planes)
    grad_x = z_stencil(y_smoothed[:, :, cross_width:], smooth_taps, planes)
    return (grad_z, grad_y, grad_x)


def shape_table(edge_len):
    position = (jnp.arange(edge_len).astype(jnp.float32) + 0.5) / edge_len
    return jnp.stack([1.0 - position, position], axis=1)


def layer_terms(padded, z_start, ref_layer, grad_layer, node_pair, layer_offsets):
    edge_len = ref_layer.shape[0]
    cross_width = ref_layer.shape[1]
    per_row = cross_width // edge_len
    ref_blocks = ref_layer.reshape(edge_len, per_row, edge_len, per_row, edge_len).transpose(
        1, 3, 0, 2, 4
    )
    ref_blocks = ref_blocks.reshape(per_row * per_row, edge_len, edge_len, edge_len)
    grad_blocks = grad_layer.reshape(3, edge_len, per_row, edge_len, per_row, edge_len).transpose(
        2, 4, 0, 1, 3, 5
    )
    grad_blocks = grad_blocks.reshape(per_row * per_row, 3, edge_len, edge_len, edge_len)
    picked_nodes = []
    for j in range(2):
        for k in range(2):
            picked_nodes.append(node_pair[:, :, j : j + per_row, k : k + per_row])
    corner_nodes = jnp.stack(picked_nodes, axis=2).reshape(3, 2, 2, 2, per_row, per_row)
    corner_nodes = corner_nodes.transpose(4, 5, 0, 1, 2, 3).reshape(per_row * per_row, 3, 2, 2, 2)
    element_ids = jnp.arange(per_row * per_row, dtype=jnp.int32)
    starts_z = z_start + layer_offsets[0] + HALO
    starts_y = element_ids // per_row * edge_len + layer_offsets[1] + HALO
    starts_x = element_ids % per_row * edge_len + layer_offsets[2] + HALO

    def cut_window(start_z, start_y, start_x):
        return lax.dynamic_slice(
            padded, (start_z, start_y, start_x), (edge_len + 1, edge_len + 1, edge_len + 1)
        )

    windows = jax.vmap(cut_window)(starts_z, starts_y, starts_x).astype(jnp.float32)
    shapes = shape_table(edge_len)
    subvoxel_field = jnp.einsum(
        "enijk,ai,bj,ck->enabc",
        corner_nodes,
        shapes,
        shapes,
        shapes,
        precision=lax.Precision.HIGHEST,
    )
    warped = jnp.zeros((per_row * per_row, edge_len, edge_len, edge_len), jnp.float32)
    for corner_z in range(2):
        weight_z = subvoxel_field[:, 0] if corner_z else 1.0 - subvoxel_field[:, 0]
        for corner_y in range(2):
            weight_y = subvoxel_field[:, 1] if corner_y else 1.0 - subvoxel_field[:, 1]
            for corner_x in range(2):
                weight_x = subvoxel_field[:, 2] if corner_x else 1.0 - subvoxel_field[:, 2]
                sample = windows[
                    :,
                    corner_z : corner_z + edge_len,
                    corner_y : corner_y + edge_len,
                    corner_x : corner_x + edge_len,
                ]
                warped = warped + weight_z * weight_y * weight_x * sample
    misfit = warped - ref_blocks.astype(jnp.float32)
    products = grad_blocks.astype(jnp.float32) * misfit[:, None]
    element_rhs = jnp.einsum(
        "enabc,ai,bj,ck->enijk", products, shapes, shapes, shapes, precision=lax.Precision.HIGHEST
    ) * (1.0 / edge_len)
    misfit_layer = misfit.reshape(per_row, per_row, edge_len, edge_len, edge_len).transpose(
        2, 0, 3, 1, 4
    )
    misfit_layer = misfit_layer.reshape(edge_len, cross_width, cross_width)
    corner_sums = element_rhs.reshape(per_row, per_row, 3, 2, 2, 2)
    planes = jnp.zeros((3, 2, per_row + 1, per_row + 1), jnp.float32)
    for j in range(2):
        for k in range(2):
            placed = corner_sums[:, :, :, :, j, k].transpose(2, 3, 0, 1)
            planes = planes + jnp.pad(placed, ((0, 0), (0, 0), (j, 1 - j), (k, 1 - k)))
    return (misfit_layer, planes.reshape(3, 2, (per_row + 1) * (per_row + 1)))


def body(tomogram, deformed, subvoxel, offsets):
    ref_slab = lax.all_gather(tomogram, "scan", axis=0, tiled=True)
    extended = padded_2(ref_slab, (("brick", 0),), RADIUS)
    grad_z, grad_y, grad_x = gradients(extended)
    gradient_all = jnp.stack([grad_z, grad_y, grad_x])
    node_above = passed_along(subvoxel, "brick", -1)
    nodes_all = jnp.concatenate([subvoxel, node_above], axis=2)
    rimmed = padded_2(deformed, (("brick", 1),), HALO)
    padded_all = jnp.pad(rimmed, ((0, 0), (0, 0), (HALO, HALO), (HALO, HALO)))
    cross_width = tomogram.shape[1]
    per_row = cross_width // E
    layers = ref_slab.shape[0] // E

    def one_scan(scan_items):
        padded, node_values, scan_offsets = scan_items
        node_grid = node_values.reshape(3, layers + 1, per_row + 1, per_row + 1)

        def one_layer(layer_index):
            return layer_terms(
                padded, layer_index * E, ref_slab, gradient_all, node_grid, scan_offsets
            )

        misfits, planes = lax.map(one_layer, jnp.arange(layers, dtype=jnp.int32))
        residual_scan = misfits.reshape(layers * E, cross_width, cross_width).astype(jnp.bfloat16)
        zero_plane = jnp.zeros((1, 3, planes.shape[-1]), jnp.float32)
        stacked = jnp.concatenate([planes[:, :, 0], zero_plane], axis=0) + jnp.concatenate(
            [zero_plane, planes[:, :, 1]], axis=0
        )
        return (residual_scan, stacked.transpose(1, 0, 2))

    residual_map, local_rhs = lax.map(one_scan, (padded_all, nodes_all, offsets))
    passed = passed_along(local_rhs[:, :, layers:], "brick", 1)
    node_rhs = local_rhs[:, :, :layers] + jnp.concatenate(
        [passed, jnp.zeros_like(local_rhs[:, :, 1:layers])], axis=2
    )
    return (residual_map, node_rhs)


def solution(mesh):
    return jax.shard_map(
        body,
        mesh=mesh,
        in_specs=(
            P(("brick", "scan"), None, None),
            P("scan", "brick", None, None),
            P("scan", None, "brick", None),
            P("scan", None, "brick"),
        ),
        out_specs=(P("scan", "brick", None, None), P("scan", None, "brick", None)),
        check_vma=False,
    )
```

profile of v0, /device:TPU:70, one launch (start us, length us, event | category | flops | bytes accessed | tf_op | source)
XLA Modules:
  0.0 354.6 jit_solution(18376039902675445702)
XLA Ops:
  7.2 0.7 all-gather.2.cloned.1.call-update
  7.9 1.3 fusion.67
  9.2 6.2 %collective-permute-start.2 = (bf16[1,16,128,128]{3,2,1,0:T(8,128)(2,1)S(1)}, bf16[1,16,128,128]{3,2,1,0:T(8,128)(2,1)S(1)}, u32[]{:S(2)}, u32[]{:S(2)}) collective-permute-start(bf16[1,16,128,128]{3,2,1,0:T(8,128)(2,1)S(1)} %get-tuple-element.82), channel_id=1, source_target_pairs={{4,0},{8,4},{12,8},{16,12},{20,16},{24,20},{28,24},{32,28},{36,32}... | collective-permute-start | bytes 1572872 | tf_op jit(solution)/shard_map/ppermute | solution.py:24
  15.4 1.9 collective-permute-start.1
  17.4 6.9 %collective-permute-start = (f32[1,3,1,25]{3,2,1,0:T(1,128)}, f32[1,3,1,25]{3,2,1,0:T(1,128)S(1)}, u32[]{:S(2)}, u32[]{:S(2)}) collective-permute-start(f32[1,3,1,25]{3,2,1,0:T(1,128)} %param.6), channel_id=1, source_target_pairs={{4,0},{8,4},{12,8},{16,12},{20,16},{24,20},{28,24},{32,28},{36,32}... | collective-permute-start | bytes 908 | tf_op jit(solution)/shard_map/ppermute | solution.py:34
  24.3 0.6 multiply_reduce_fusion
  24.9 0.6 fusion.44
  25.6 0.7 compare_select_fusion.2
  26.3 0.7 divide_convert_fusion.1
  26.9 0.7 fusion.70
  32.1 0.6 divide_convert_fusion
  32.8 0.7 fusion.69
  38.0 0.7 pad_maximum_fusion.2
  39.4 2.7 fusion.24
  42.1 43.1 %convolution_bitcast_fusion = f32[16,3,32,32,32]{4,3,1,0,2:T(8,128)} fusion(f32[32,16,3,2,32]{4,0,3,2,1:T(8,128)S(1)} %fusion.24, f32[32,1]{0,1:T(1,128)S(1)} %get-tuple-element.110, f32[32,1]{0,1:T(1,128)S(1)} %get-tuple-element.111), kind=kOutput, calls=%fused_computation.13 | convolution fusion | flops 37748800 | bytes 6684928 | tf_op jit(solution)/shard_map/while/body/eval_jaxpr/while/body/eval_jaxpr/enijk,ai,bj,ck->enabc/dot_general | solution.py:124
  85.2 8.0 %fusion.13 = bf16[64,160,160]{2,1,0:T(8,128)(2,1)} fusion(bf16[1,16,128,128]{3,2,1,0:T(8,128)(2,1)S(1)} %collective-permute-done.2, bf16[1,32,128,128]{3,2,1,0:T(8,128)(2,1)S(1)} %copy-done.1, bf16[1,16,128,128]{3,2,1,0:T(8,128)(2,1)S(1)} %collective-permute-done.1), kind=kLoop, calls=%fused_computation.37 | loop fusion | flops 31129600 | bytes 5373952 | tf_op jit(solution)/shard_map/while/body/jit(dynamic_index_in_dim)/squeeze | solution.py:194
  93.2 77.1 %while.4 = (s32[]{:T(128)}, bf16[64,160,160]{2,1,0:T(8,128)(2,1)}, s32[16,3]{0,1:T(4,128)S(1)}, bf16[16,33,33,33]{3,2,0,1:T(8,128)(2,1)}, s32[]{:T(128)}) while((s32[]{:T(128)}, bf16[64,160,160]{2,1,0:T(8,128)(2,1)}, s32[16,3]{0,1:T(4,128)S(1)}, bf16[16,33,33,33]{3,2,0,1:T(8,128)(2,1)}, s32[]{:T(128)}) %tuple.55), condition=%wide.while_cond, body=%wide.while_body.sunk | while | flops 2 | bytes 677501 | solution.py:118
  93.3 0.6 fusion.77
  93.9 4.2 %bitcast_dynamic-update-slice_fusion.2 = bf16[16,33,33,33]{3,2,0,1:T(8,128)(2,1)} fusion(bf16[16,33,33,33]{3,2,0,1:T(8,128)(2,1)} %get-tuple-element.153, s32[]{:T(128)S(6)} %copy.86, bf16[64,160,160]{2,1,0:T(8,128)(2,1)} %get-tuple-element.156, s32[]{:T(128)} %bitcast.159, s32[]{:T(128)} %bitcast.160, s32[]{:T(128)} %bitcast.161), kind=kLoop, calls=%fused_computation.clone.1 | loop fusion | bytes 677380 | tf_op jit(solution)/shard_map/while/body/eval_jaxpr/while/body/eval_jaxpr/vmap()/gather
  98.2 0.6 fusion.77
  98.8 4.1 %bitcast_dynamic-update-slice_fusion.2 = bf16[16,33,33,33]{3,2,0,1:T(8,128)(2,1)} fusion(bf16[16,33,33,33]{3,2,0,1:T(8,128)(2,1)} %get-tuple-element.153, s32[]{:T(128)S(6)} %copy.86, bf16[64,160,160]{2,1,0:T(8,128)(2,1)} %get-tuple-element.156, s32[]{:T(128)} %bitcast.159, s32[]{:T(128)} %bitcast.160, s32[]{:T(128)} %bitcast.161), kind=kLoop, calls=%fused_computation.clone.1 | loop fusion | bytes 677380 | tf_op jit(solution)/shard_map/while/body/eval_jaxpr/while/body/eval_jaxpr/vmap()/gather
  103.6 4.1 %bitcast_dynamic-update-slice_fusion.2 = bf16[16,33,33,33]{3,2,0,1:T(8,128)(2,1)} fusion(bf16[16,33,33,33]{3,2,0,1:T(8,128)(2,1)} %get-tuple-element.153, s32[]{:T(128)S(6)} %copy.86, bf16[64,160,160]{2,1,0:T(8,128)(2,1)} %get-tuple-element.156, s32[]{:T(128)} %bitcast.159, s32[]{:T(128)} %bitcast.160, s32[]{:T(128)} %bitcast.161), kind=kLoop, calls=%fused_computation.clone.1 | loop fusion | bytes 677380 | tf_op jit(solution)/shard_map/while/body/eval_jaxpr/while/body/eval_jaxpr/vmap()/gather
  107.7 0.6 fusion.77
  108.3 4.2 %bitcast_dynamic-update-slice_fusion.2 = bf16[16,33,33,33]{3,2,0,1:T(8,128)(2,1)} fusion(bf16[16,33,33,33]{3,2,0,1:T(8,128)(2,1)} %get-tuple-element.153, s32[]{:T(128)S(6)} %copy.86, bf16[64,160,160]{2,1,0:T(8,128)(2,1)} %get-tuple-element.156, s32[]{:T(128)} %bitcast.159, s32[]{:T(128)} %bitcast.160, s32[]{:T(128)} %bitcast.161), kind=kLoop, calls=%fused_computation.clone.1 | loop fusion | bytes 677380 | tf_op jit(solution)/shard_map/while/body/eval_jaxpr/while/body/eval_jaxpr/vmap()/gather
  112.6 0.6 fusion.77
  113.2 4.1 %bitcast_dynamic-update-slice_fusion.2 = bf16[16,33,33,33]{3,2,0,1:T(8,128)(2,1)} fusion(bf16[16,33,33,33]{3,2,0,1:T(8,128)(2,1)} %get-tuple-element.153, s32[]{:T(128)S(6)} %copy.86, bf16[64,160,160]{2,1,0:T(8,128)(2,1)} %get-tuple-element.156, s32[]{:T(128)} %bitcast.159, s32[]{:T(128)} %bitcast.160, s32[]{:T(128)} %bitcast.161), kind=kLoop, calls=%fused_computation.clone.1 | loop fusion | bytes 677380 | tf_op jit(solution)/shard_map/while/body/eval_jaxpr/while/body/eval_jaxpr/vmap()/gather
  117.4 0.6 fusion.77
  118.0 4.2 %bitcast_dynamic-update-slice_fusion.2 = bf16[16,33,33,33]{3,2,0,1:T(8,128)(2,1)} fusion(bf16[16,33,33,33]{3,2,0,1:T(8,128)(2,1)} %get-tuple-element.153, s32[]{:T(128)S(6)} %copy.86, bf16[64,160,160]{2,1,0:T(8,128)(2,1)} %get-tuple-element.156, s32[]{:T(128)} %bitcast.159, s32[]{:T(128)} %bitcast.160, s32[]{:T(128)} %bitcast.161), kind=kLoop, calls=%fused_computation.clone.1 | loop fusion | bytes 677380 | tf_op jit(solution)/shard_map/while/body/eval_jaxpr/while/body/eval_jaxpr/vmap()/gather
  122.2 0.6 fusion.77
  122.8 4.1 %bitcast_dynamic-update-slice_fusion.2 = bf16[16,33,33,33]{3,2,0,1:T(8,128)(2,1)} fusion(bf16[16,33,33,33]{3,2,0,1:T(8,128)(2,1)} %get-tuple-element.153, s32[]{:T(128)S(6)} %copy.86, bf16[64,160,160]{2,1,0:T(8,128)(2,1)} %get-tuple-element.156, s32[]{:T(128)} %bitcast.159, s32[]{:T(128)} %bitcast.160, s32[]{:T(128)} %bitcast.161), kind=kLoop, calls=%fused_computation.clone.1 | loop fusion | bytes 677380 | tf_op jit(solution)/shard_map/while/body/eval_jaxpr/while/body/eval_jaxpr/vmap()/gather
  127.6 4.1 %bitcast_dynamic-update-slice_fusion.2 = bf16[16,33,33,33]{3,2,0,1:T(8,128)(2,1)} fusion(bf16[16,33,33,33]{3,2,0,1:T(8,128)(2,1)} %get-tuple-element.153, s32[]{:T(128)S(6)} %copy.86, bf16[64,160,160]{2,1,0:T(8,128)(2,1)} %get-tuple-element.156, s32[]{:T(128)} %bitcast.159, s32[]{:T(128)} %bitcast.160, s32[]{:T(128)} %bitcast.161), kind=kLoop, calls=%fused_computation.clone.1 | loop fusion | bytes 677380 | tf_op jit(solution)/shard_map/while/body/eval_jaxpr/while/body/eval_jaxpr/vmap()/gather
  132.4 4.1 %bitcast_dynamic-update-slice_fusion.2 = bf16[16,33,33,33]{3,2,0,1:T(8,128)(2,1)} fusion(bf16[16,33,33,33]{3,2,0,1:T(8,128)(2,1)} %get-tuple-element.153, s32[]{:T(128)S(6)} %copy.86, bf16[64,160,160]{2,1,0:T(8,128)(2,1)} %get-tuple-element.156, s32[]{:T(128)} %bitcast.159, s32[]{:T(128)} %bitcast.160, s32[]{:T(128)} %bitcast.161), kind=kLoop, calls=%fused_computation.clone.1 | loop fusion | bytes 677380 | tf_op jit(solution)/shard_map/while/body/eval_jaxpr/while/body/eval_jaxpr/vmap()/gather
  137.2 4.1 %bitcast_dynamic-update-slice_fusion.2 = bf16[16,33,33,33]{3,2,0,1:T(8,128)(2,1)} fusion(bf16[16,33,33,33]{3,2,0,1:T(8,128)(2,1)} %get-tuple-element.153, s32[]{:T(128)S(6)} %copy.86, bf16[64,160,160]{2,1,0:T(8,128)(2,1)} %get-tuple-element.156, s32[]{:T(128)} %bitcast.159, s32[]{:T(128)} %bitcast.160, s32[]{:T(128)} %bitcast.161), kind=kLoop, calls=%fused_computation.clone.1 | loop fusion | bytes 677380 | tf_op jit(solution)/shard_map/while/body/eval_jaxpr/while/body/eval_jaxpr/vmap()/gather
  142.1 4.1 %bitcast_dynamic-update-slice_fusion.2 = bf16[16,33,33,33]{3,2,0,1:T(8,128)(2,1)} fusion(bf16[16,33,33,33]{3,2,0,1:T(8,128)(2,1)} %get-tuple-element.153, s32[]{:T(128)S(6)} %copy.86, bf16[64,160,160]{2,1,0:T(8,128)(2,1)} %get-tuple-element.156, s32[]{:T(128)} %bitcast.159, s32[]{:T(128)} %bitcast.160, s32[]{:T(128)} %bitcast.161), kind=kLoop, calls=%fused_computation.clone.1 | loop fusion | bytes 677380 | tf_op jit(solution)/shard_map/while/body/eval_jaxpr/while/body/eval_jaxpr/vmap()/gather
  146.9 4.2 %bitcast_dynamic-update-slice_fusion.2 = bf16[16,33,33,33]{3,2,0,1:T(8,128)(2,1)} fusion(bf16[16,33,33,33]{3,2,0,1:T(8,128)(2,1)} %get-tuple-element.153, s32[]{:T(128)S(6)} %copy.86, bf16[64,160,160]{2,1,0:T(8,128)(2,1)} %get-tuple-element.156, s32[]{:T(128)} %bitcast.159, s32[]{:T(128)} %bitcast.160, s32[]{:T(128)} %bitcast.161), kind=kLoop, calls=%fused_computation.clone.1 | loop fusion | bytes 677380 | tf_op jit(solution)/shard_map/while/body/eval_jaxpr/while/body/eval_jaxpr/vmap()/gather
  151.7 4.2 %bitcast_dynamic-update-slice_fusion.2 = bf16[16,33,33,33]{3,2,0,1:T(8,128)(2,1)} fusion(bf16[16,33,33,33]{3,2,0,1:T(8,128)(2,1)} %get-tuple-element.153, s32[]{:T(128)S(6)} %copy.86, bf16[64,160,160]{2,1,0:T(8,128)(2,1)} %get-tuple-element.156, s32[]{:T(128)} %bitcast.159, s32[]{:T(128)} %bitcast.160, s32[]{:T(128)} %bitcast.161), kind=kLoop, calls=%fused_computation.clone.1 | loop fusion | bytes 677380 | tf_op jit(solution)/shard_map/while/body/eval_jaxpr/while/body/eval_jaxpr/vmap()/gather
  156.6 4.2 %bitcast_dynamic-update-slice_fusion.2 = bf16[16,33,33,33]{3,2,0,1:T(8,128)(2,1)} fusion(bf16[16,33,33,33]{3,2,0,1:T(8,128)(2,1)} %get-tuple-element.153, s32[]{:T(128)S(6)} %copy.86, bf16[64,160,160]{2,1,0:T(8,128)(2,1)} %get-tuple-element.156, s32[]{:T(128)} %bitcast.159, s32[]{:T(128)} %bitcast.160, s32[]{:T(128)} %bitcast.161), kind=kLoop, calls=%fused_computation.clone.1 | loop fusion | bytes 677380 | tf_op jit(solution)/shard_map/while/body/eval_jaxpr/while/body/eval_jaxpr/vmap()/gather
  161.4 4.1 %bitcast_dynamic-update-slice_fusion.2 = bf16[16,33,33,33]{3,2,0,1:T(8,128)(2,1)} fusion(bf16[16,33,33,33]{3,2,0,1:T(8,128)(2,1)} %get-tuple-element.153, s32[]{:T(128)S(6)} %copy.86, bf16[64,160,160]{2,1,0:T(8,128)(2,1)} %get-tuple-element.156, s32[]{:T(128)} %bitcast.159, s32[]{:T(128)} %bitcast.160, s32[]{:T(128)} %bitcast.161), kind=kLoop, calls=%fused_computation.clone.1 | loop fusion | bytes 677380 | tf_op jit(solution)/shard_map/while/body/eval_jaxpr/while/body/eval_jaxpr/vmap()/gather
  166.2 4.2 %bitcast_dynamic-update-slice_fusion.2 = bf16[16,33,33,33]{3,2,0,1:T(8,128)(2,1)} fusion(bf16[16,33,33,33]{3,2,0,1:T(8,128)(2,1)} %get-tuple-element.153, s32[]{:T(128)S(6)} %copy.86, bf16[64,160,160]{2,1,0:T(8,128)(2,1)} %get-tuple-element.156, s32[]{:T(128)} %bitcast.159, s32[]{:T(128)} %bitcast.160, s32[]{:T(128)} %bitcast.161), kind=kLoop, calls=%fused_computation.clone.1 | loop fusion | bytes 677380 | tf_op jit(solution)/shard_map/while/body/eval_jaxpr/while/body/eval_jaxpr/vmap()/gather
  170.4 7.9 %convert_element_type.294 = f32[16,33,33,33]{3,2,0,1:T(8,128)} convert(bf16[16,33,33,33]{3,2,0,1:T(8,128)(2,1)} %get-tuple-element.65) | non-fusion elementwise | flops 574992 | bytes 3449952 | tf_op jit(solution)/shard_map/while/body/eval_jaxpr/while/body/eval_jaxpr/convert_element_type | solution.py:122
  178.3 7.1 %reshape.306 = f32[32,4,32,4,32]{4,3,2,1,0:T(4,128)} reshape(bf16[32,128,128]{2,1,0:T(8,128)(2,1)} %all-gather.2.cloned.1.call-done) | data formatting | bytes 3145728 | tf_op jit(solution)/shard_map/while/body/eval_jaxpr/while/body/eval_jaxpr/convert_element_type | solution.py:146
  185.4 8.0 %copy.37 = f32[32,4,32,4,32]{4,2,3,1,0:T(8,128)} copy(f32[32,4,32,4,32]{4,3,2,1,0:T(4,128)} %reshape.306) | data formatting | bytes 4194304 | tf_op jit(solution)/shard_map/while/body/eval_jaxpr/while/body/eval_jaxpr/convert_element_type | solution.py:146
  193.3 2.0 collective-permute-start.4
  195.3 3.9 %collective-permute-start.3 = (bf16[3,128,128]{2,1,0:T(8,128)(2,1)S(1)}, bf16[3,128,128]{2,1,0:T(8,128)(2,1)S(1)}, u32[]{:S(2)}, u32[]{:S(2)}) collective-permute-start(bf16[3,128,128]{2,1,0:T(8,128)(2,1)S(1)} %get-tuple-element.79), channel_id=1, source_target_pairs={{0,4},{4,8},{8,12},{12,16},{16,20},{20,24},{24,28},{28,32},{32,36}... | collective-permute-start | bytes 294920 | tf_op jit(solution)/shard_map/ppermute | solution.py:22
  199.2 43.0 %fusion.63 = (bf16[16,32,32,32]{3,2,0,1:T(8,128)(2,1)}, f32[16,32,32,32]{3,2,0,1:T(8,128)}) fusion(f32[16,32,32,32]{3,2,0,1:T(8,128)} %bitcast.164, f32[16,33,33,33]{3,2,0,1:T(8,128)} %convert_element_type.294, f32[16,3,32,32,32]{4,3,1,0,2:T(8,128)} %convolution_bitcast_fusion), kind=kLoop, calls=%fused_computation.131 | loop fusion | flops 16777216 | bytes 28311552 | tf_op jit(solution)/shard_map/while/body/eval_jaxpr/convert_element_type | solution.py:187
  242.4 0.8 convolution_convert_fusion
  243.2 0.8 convert_bitcast_fusion
  244.6 1.5 add_convert_fusion
  246.1 1.5 add_convert_fusion.2
  247.6 3.2 stack.56
  250.8 5.0 %copy.41 = bf16[1,32,4,32,4,32]{5,3,1,0,4,2:T(8,128)(2,1)} copy(bf16[1,32,4,32,4,32]{5,4,3,2,1,0:T(4,128)(2,1)} %stack.56) | data formatting | bytes 2097152 | tf_op jit(solution)/shard_map/stack | solution.py:168
  255.9 1.6 add_convert_fusion.1
  257.5 3.2 stack.55
  260.7 4.9 %copy.40 = bf16[1,32,4,32,4,32]{5,3,1,0,4,2:T(8,128)(2,1)} copy(bf16[1,32,4,32,4,32]{5,4,3,2,1,0:T(4,128)(2,1)} %stack.55) | data formatting | bytes 2097152 | tf_op jit(solution)/shard_map/stack | solution.py:168
  265.6 3.3 stack.54
  268.9 5.1 %copy.39 = bf16[1,32,4,32,4,32]{5,3,1,0,4,2:T(8,128)(2,1)} copy(bf16[1,32,4,32,4,32]{5,4,3,2,1,0:T(4,128)(2,1)} %stack.54) | data formatting | bytes 2097152 | tf_op jit(solution)/shard_map/stack | solution.py:168
  274.0 7.9 %maximum_convert_fusion = f32[3,32,4,32,4,32]{5,3,1,0,4,2:T(8,128)S(1)} fusion(bf16[1,32,4,32,4,32]{5,3,1,0,4,2:T(8,128)(2,1)} %copy.41, bf16[1,32,4,32,4,32]{5,3,1,0,4,2:T(8,128)(2,1)} %copy.40, bf16[1,32,4,32,4,32]{5,3,1,0,4,2:T(8,128)(2,1)} %copy.39), kind=kLoop, calls=%fused_computation.9 | loop fusion | flops 4718592 | bytes 9437184 | tf_op jit(solution)/shard_map/while/body/eval_jaxpr/while/body/eval_jaxpr/convert_element_type | solution.py:147
  281.9 13.3 %bitcast_multiply_fusion = f32[16,3,32,32,32]{4,3,2,1,0:T(8,128)} fusion(f32[3,32,4,32,4,32]{5,3,1,0,4,2:T(8,128)S(1)} %maximum_convert_fusion, f32[16,32,32,32]{3,2,0,1:T(8,128)S(1)} %bitcast.163), kind=kLoop, calls=%fused_computation.2 | loop fusion | flops 1572864 | bytes 14680064 | tf_op jit(solution)/shard_map/while/body/eval_jaxpr/while/body/eval_jaxpr/mul | solution.py:147
  295.2 32.8 %fusion = f32[2,16,3,32,32]{4,0,3,2,1:T(2,128)S(1)} fusion(f32[16,3,32,32,32]{4,3,2,1,0:T(8,128)} %bitcast_multiply_fusion, f32[32,1]{0,1:T(1,128)S(1)} %get-tuple-element.110, f32[32,1]{0,1:T(1,128)S(1)} %get-tuple-element.111), kind=kOutput, calls=%fused_computation.3 | convolution fusion | flops 37748800 | bytes 6684928 | tf_op jit(solution)/shard_map/while/body/eval_jaxpr/while/body/eval_jaxpr/enabc,ai,bj,ck->enijk/dot_general | solution.py:148
  328.0 0.9 fusion.17
  329.0 0.8 fusion.22
  330.2 2.2 collective-permute-start.5
  332.3 8.4 %copy.38 = bf16[32,4,32,4,32]{4,3,2,1,0:T(4,128)(2,1)} copy(bf16[32,4,32,4,32]{4,2,3,1,0:T(8,128)(2,1)} %bitcast.167) | data formatting | bytes 2097152 | tf_op jit(solution)/shard_map/while/body/eval_jaxpr/convert_element_type | solution.py:187
  340.7 6.0 %convert_element_type.302 = bf16[1,32,128,128]{3,2,1,0:T(8,128)(2,1)} reshape(bf16[32,4,32,4,32]{4,3,2,1,0:T(4,128)(2,1)} %copy.38) | data formatting | bytes 2097152 | tf_op jit(solution)/shard_map/while/body/eval_jaxpr/convert_element_type | solution.py:187
  (68 shorter events, 9.6 us)
Async XLA Ops:
  7.2 171.1 %all-gather.2.cloned.1.call-start = ((), (), s32[]{:S(2)}) async-start(), calls=%async_computation | async-start | bytes 1310720 | tf_op jit(solution)/shard_map/all_gather | solution.py:165
  9.2 76.0 %collective-permute-start.2 = (bf16[1,16,128,128]{3,2,1,0:T(8,128)(2,1)S(1)}, bf16[1,16,128,128]{3,2,1,0:T(8,128)(2,1)S(1)}, u32[]{:S(2)}, u32[]{:S(2)}) collective-permute-start(bf16[1,16,128,128]{3,2,1,0:T(8,128)(2,1)S(1)} %get-tuple-element.82), channel_id=1, source_target_pairs={{4,0},{8,4},{12,8},{16,12},{20,16},{24,20},{28,24},{32,28},{36,32}... | collective-permute-start | bytes 1572872 | tf_op jit(solution)/shard_map/ppermute | solution.py:24
  15.4 69.8 %collective-permute-start.1 = (bf16[1,16,128,128]{3,2,1,0:T(8,128)(2,1)S(1)}, bf16[1,16,128,128]{3,2,1,0:T(8,128)(2,1)S(1)}, u32[]{:S(2)}, u32[]{:S(2)}) collective-permute-start(bf16[1,16,128,128]{3,2,1,0:T(8,128)(2,1)S(1)} %get-tuple-element.81), channel_id=1, source_target_pairs={{0,4},{4,8},{8,12},{12,16},{16,20},{20,24},{24,28},{28,32},{32,36}... | collective-permute-start | bytes 1572872 | tf_op jit(solution)/shard_map/ppermute | solution.py:22
  17.4 20.7 %collective-permute-start = (f32[1,3,1,25]{3,2,1,0:T(1,128)}, f32[1,3,1,25]{3,2,1,0:T(1,128)S(1)}, u32[]{:S(2)}, u32[]{:S(2)}) collective-permute-start(f32[1,3,1,25]{3,2,1,0:T(1,128)} %param.6), channel_id=1, source_target_pairs={{4,0},{8,4},{12,8},{16,12},{20,16},{24,20},{28,24},{32,28},{36,32}... | collective-permute-start | bytes 908 | tf_op jit(solution)/shard_map/ppermute | solution.py:34
  42.1 43.1 %copy-start.1 = (bf16[1,32,128,128]{3,2,1,0:T(8,128)(2,1)S(1)}, bf16[1,32,128,128]{3,2,1,0:T(8,128)(2,1)}, u32[]{:S(2)}) copy-start(bf16[1,32,128,128]{3,2,1,0:T(8,128)(2,1)} %param.5) | copy-start | bytes 3145732
  185.4 8.0 %copy-start = (bf16[32,128,128]{2,1,0:T(8,128)(2,1)S(1)}, bf16[32,128,128]{2,1,0:T(8,128)(2,1)}, u32[]{:S(2)}) copy-start(bf16[32,128,128]{2,1,0:T(8,128)(2,1)} %all-gather.2.cloned.1.call-done) | copy-start | bytes 3145732
  193.3 48.9 %collective-permute-start.4 = (bf16[3,128,128]{2,1,0:T(8,128)(2,1)S(1)}, bf16[3,128,128]{2,1,0:T(8,128)(2,1)S(1)}, u32[]{:S(2)}, u32[]{:S(2)}) collective-permute-start(bf16[3,128,128]{2,1,0:T(8,128)(2,1)S(1)} %get-tuple-element.80), channel_id=1, source_target_pairs={{4,0},{8,4},{12,8},{16,12},{20,16},{24,20},{28,24},{32,28},{36,32}... | collective-permute-start | bytes 294920 | tf_op jit(solution)/shard_map/ppermute | solution.py:24
  195.3 46.9 %collective-permute-start.3 = (bf16[3,128,128]{2,1,0:T(8,128)(2,1)S(1)}, bf16[3,128,128]{2,1,0:T(8,128)(2,1)S(1)}, u32[]{:S(2)}, u32[]{:S(2)}) collective-permute-start(bf16[3,128,128]{2,1,0:T(8,128)(2,1)S(1)} %get-tuple-element.79), channel_id=1, source_target_pairs={{0,4},{4,8},{8,12},{12,16},{16,20},{20,24},{24,28},{28,32},{32,36}... | collective-permute-start | bytes 294920 | tf_op jit(solution)/shard_map/ppermute | solution.py:22
  268.9 12.9 %slice-start = ((s8[8388608]{0:T(1024)(128)(4,1)}), s8[4194304]{0:T(1024)(128)(4,1)S(1)}, s32[]{:S(2)}) async-start(s8[8388608]{0:T(1024)(128)(4,1)} %bitcast.162), calls=%async_computation.1 | async-start | bytes 8388608
  274.0 7.9 %slice-start.1 = ((s8[8388608]{0:T(1024)(128)(4,1)}), s8[4194304]{0:T(1024)(128)(4,1)S(1)}, s32[]{:S(2)}) async-start(s8[8388608]{0:T(1024)(128)(4,1)} %bitcast.162), calls=%async_computation.2 | async-start | bytes 8388608
  330.2 16.6 %collective-permute-start.5 = (f32[1,3,1,25]{3,2,1,0:T(1,128)S(1)}, f32[1,3,1,25]{3,2,1,0:T(1,128)S(1)}, u32[]{:S(2)}, u32[]{:S(2)}) collective-permute-start(f32[1,3,1,25]{3,2,1,0:T(1,128)S(1)} %slice.422), channel_id=1, source_target_pairs={{0,4},{4,8},{8,12},{12,16},{16,20},{20,24},{24,28},{28,32},{32,36}... | collective-permute-start | bytes 908 | tf_op jit(solution)/shard_map/ppermute | solution.py:34
Sparse Core Ops, SparseCore 0:
  9.7 27.9 all-gather.1
where the time goes:
time: 361 us; the launch traced here: 355 us
  local copies, waits for them, and re-layouts  135 us (37%)
  other arithmetic  89.6 us (25%)
  matrix products  82.8 us (23%)
  between operations  23.8 us (7%)
  starting transfers between devices  23.2 us (6%)
    gather x48, local copies, waits for them, and re-layouts  77.1 us
    dot_general x3, matrix products, layer_terms(): jnp.einsum('enijk,ai,bj,ck->enabc', corner_nodes, shapes, shapes, shapes,...  46.2 us
    convert_element_type x1, other arithmetic, one_scan(): misfits.reshape(layers * E, cross_width, cross_width).astype(jnp.bfloat16)  43 us
    dot_general x3, matrix products, layer_terms(): jnp.einsum('enabc,ai,bj,ck->enijk', products, shapes, shapes, shapes, pre...  34.5 us
    another operation x6, local copies, waits for them, and re-layouts, body(): gradient_all = jnp.stack([grad_z, grad_y, grad_x])  24.8 us
    convert_element_type x2, local copies, waits for them, and re-layouts, layer_terms(): misfit = warped - ref_blocks.astype(jnp.float32)  15.1 us
    convert_element_type x2, local copies, waits for them, and re-layouts, one_scan(): misfits.reshape(layers * E, cross_width, cross_width).astype(jnp.bfloat16)  14.4 us
    mul x1, other arithmetic, layer_terms(): products = grad_blocks.astype(jnp.float32) * misfit[:, None]  13.3 us
  transfers between devices with their start and end apart: 7, of which 0 were waited for; matrix products, arithmetic and copies ran while one was open for 57% of the time, Pallas kernels for 0%

commit v1 on v0

v1 whole, which is shorter than its diff:
```python
import functools

import jax
import jax.numpy as jnp
import ml_dtypes
import numpy as np
from jax import lax
from jax.experimental import pallas as pl
from jax.experimental.pallas import tpu as pltpu
from jax.sharding import PartitionSpec as P

E = 32
HALO = 16
RADIUS = 3
NXY = 128
PER_ROW = 4
NODES = 5
GAUSS_SIGMA = 1.0

WIN = 40
WPLANES = 34
VPLANES = E + 2 * HALO
YPAD = HALO
VROWS = 168
GROUP = 4


def filter_taps():
    tap_pos = np.arange(-RADIUS, RADIUS + 1).astype(np.float32)
    gaussian = np.exp(-tap_pos * tap_pos / np.float32(2.0 * GAUSS_SIGMA * GAUSS_SIGMA))
    smooth = gaussian / np.sum(gaussian)
    slope = tap_pos * gaussian / np.sum(tap_pos * tap_pos * gaussian)
    return (
        [float(v) for v in smooth.astype(ml_dtypes.bfloat16)],
        [float(v) for v in slope.astype(ml_dtypes.bfloat16)],
    )


SMOOTH, SLOPE = filter_taps()


def padded_2(cells, axis, dim, width):
    count = lax.axis_size(axis)
    ends = count - 1
    head = lax.slice_in_dim(cells, 0, width, axis=dim)
    tail = lax.slice_in_dim(cells, cells.shape[dim] - width, cells.shape[dim], axis=dim)
    return jnp.concatenate(
        [
            lax.ppermute(tail, axis, [(i, (i + 1) % count) for i in range(ends)]),
            cells,
            lax.ppermute(head, axis, [((i + 1) % count, i) for i in range(ends)]),
        ],
        axis=dim,
    )


def passed_along(block, axis, distance):
    devices = range(lax.axis_size(axis))
    route = [(i - distance, i) for i in devices if i - distance in devices]
    return lax.ppermute(block, axis, route)


def iota(shape, dim):
    return lax.broadcasted_iota(jnp.int32, shape, dim)


def band(distance, taps):
    table = jnp.zeros(distance.shape, jnp.float32)
    for tap in range(2 * RADIUS + 1):
        table = jnp.where(distance == tap - RADIUS, taps[tap], table)
    return table


def hat(shape, dim, node):
    voxel = iota(shape, dim)
    elem = voxel // E
    upper = ((voxel % E).astype(jnp.float32) + 0.5) / E
    return jnp.where(elem == node, 1.0 - upper, jnp.where(elem + 1 == node, upper, 0.0))


def filter_planes(tomo_ref, xf, grads):
    d = iota((NXY, NXY), 0) - iota((NXY, NXY), 1)
    along_x = jnp.concatenate([band(d, SMOOTH), band(d, SLOPE)], axis=1).astype(jnp.bfloat16)
    along_y = jnp.concatenate([band(-d, SMOOTH), band(-d, SLOPE)], axis=0).astype(jnp.bfloat16)
    pairs = (E + 2 * RADIUS) // 2

    def x_step(i, _):
        two = tomo_ref[pl.ds(2 * i, 2)].reshape(2 * NXY, NXY)
        out = jnp.dot(two, along_x, preferred_element_type=jnp.float32)
        xf[pl.ds(2 * i, 2)] = out.astype(jnp.bfloat16).reshape(2, NXY, 2 * NXY)
        return 0

    lax.fori_loop(0, pairs, x_step, 0)

    def y_step(i, _):
        for k in range(2):
            z = 2 * i + k
            out = jnp.dot(along_y, xf[z], preferred_element_type=jnp.float32)
            grads[0, z] = out[:NXY, :NXY]
            grads[1, z] = out[NXY:, :NXY]
            grads[2, z] = out[:NXY, NXY:]
        return 0

    lax.fori_loop(0, pairs, y_step, 0)


def spread_volume(vol_ref, volf):
    zeros_lo = jnp.zeros((YPAD, NXY), jnp.float32)
    zeros_hi = jnp.zeros((VROWS - YPAD - NXY, NXY), jnp.float32)

    def step(z, _):
        volf[z, :YPAD] = zeros_lo
        volf[z, YPAD : YPAD + NXY] = vol_ref[z].astype(jnp.float32)
        volf[z, YPAD + NXY :] = zeros_hi
        return 0

    lax.fori_loop(0, VPLANES, step, 0)


def warp_layer(offs, nodes, volf, tomo_ref, grads, lhs, win, ysum, res_ref, rhs_ref):
    ysum[...] = jnp.zeros_like(ysum)

    def element_row(ey, _):
        src = iota((NXY, NXY), 0)
        dst = iota((NXY, NXY), 1)
        blocks = []
        for ex in range(PER_ROW):
            ox = offs[2, ey * PER_ROW + ex]
            mine = dst // E == ex
            here = jnp.where(mine & (src == dst + ox), 1.0, 0.0)
            after = jnp.where(mine & (src == dst + ox + 1), 1.0, 0.0)
            blocks.append(jnp.concatenate([here, after - here], axis=1))
        shift = jnp.concatenate(blocks, axis=0).astype(jnp.bfloat16)

        def gather_planes(q, _):
            for ex in range(PER_ROW):
                oz = offs[0, ey * PER_ROW + ex] + HALO
                oy = offs[1, ey * PER_ROW + ex] + ey * E + YPAD
                two = []
                for k in range(2):
                    z = jnp.minimum(2 * q + k + oz, VPLANES - 1)
                    two.append(volf[z, pl.ds(oy, WIN), :])
                lhs[pl.ds(pl.multiple_of(q * 2 * WIN, 2 * WIN), 2 * WIN), ex * NXY : (ex + 1) * NXY] = (
                    jnp.concatenate(two, axis=0).astype(jnp.bfloat16)
                )
            return 0

        lax.fori_loop(0, WPLANES // 2, gather_planes, 0)
        rows = WPLANES * WIN
        for r0 in range(0, rows, 480):
            r1 = min(r0 + 480, rows)
            out = jnp.dot(lhs[r0:r1, :], shift, preferred_element_type=jnp.float32)
            win[0, r0:r1, :] = out[:, :NXY]
            win[1, r0:r1, :] = out[:, NXY:]

        for half in range(2):
            pb = ((iota((16, NXY), 0).astype(jnp.float32)) + (16 * half + 0.5)) / E
            start, slope = [], []
            for c in range(3):
                planes = []
                for p in range(2):
                    lo = jnp.zeros((16, NXY), jnp.float32)
                    hi = jnp.zeros((16, NXY), jnp.float32)
                    for ix in range(NODES):
                        weight = hat((16, NXY), 1, ix)
                        lo = lo + nodes(p, c, ey * NODES + ix) * weight
                        hi = hi + nodes(p, c, (ey + 1) * NODES + ix) * weight
                    planes.append(lo * (1.0 - pb) + hi * pb)
                rise = (planes[1] - planes[0]) * (1.0 / E)
                start.append(planes[0] + 0.5 * rise)
                slope.append(rise)
            yrow = pl.multiple_of(ey * E + half * 16, 16)

            def planes_step(group, carry):
                sums, prefix = list(carry[:3]), list(carry[3:])
                z0 = group * GROUP

                def corner_rows(z):
                    r = pl.multiple_of(z * WIN, 8) + 16 * half
                    return (
                        win[0, pl.ds(r, 16), :],
                        win[1, pl.ds(r, 16), :],
                        win[0, pl.ds(r + 1, 16), :],
                        win[1, pl.ds(r + 1, 16), :],
                    )

                misfits = []
                lower = corner_rows(z0)
                for k in range(GROUP):
                    z = z0 + k
                    upper = corner_rows(z + 1)
                    zf = z.astype(jnp.float32)
                    wz, wy, wx = [start[c] + zf * slope[c] for c in range(3)]

                    def in_plane(rows):
                        a = rows[0] + wx * rows[1]
                        b = rows[2] + wx * rows[3]
                        return a + wy * (b - a)

                    t0 = in_plane(lower)
                    t1 = in_plane(upper)
                    ref = tomo_ref[z + RADIUS, pl.ds(yrow, 16), :].astype(jnp.float32)
                    misfit = t0 + wz * (t1 - t0) - ref
                    res_ref[z, pl.ds(yrow, 16), :] = misfit.astype(jnp.bfloat16)
                    misfits.append(misfit)
                    lower = upper
                for c in range(3):
                    g = [grads[c, z0 + k, pl.ds(yrow, 16), :] for k in range(GROUP + 2 * RADIUS)]
                    for k in range(GROUP):
                        if c == 0:
                            grad = g[k + 4] - g[k + 2]
                            for t in (2, 3):
                                grad = grad + (SLOPE[3 + t] / SLOPE[4]) * (g[k + 3 + t] - g[k + 3 - t])
                        else:
                            grad = g[k + 3]
                            for t in (1, 2, 3):
                                grad = grad + (SMOOTH[3 + t] / SMOOTH[3]) * (g[k + 3 + t] + g[k + 3 - t])
                        sums[c] = sums[c] + grad * misfits[k]
                        prefix[c] = prefix[c] + sums[c]
                return (*sums, *prefix)

            zero = jnp.zeros((16, NXY), jnp.float32)
            done = lax.fori_loop(0, E // GROUP, planes_step, (zero,) * 6)
            for c in range(3):
                scale = (SLOPE[4] if c == 0 else SMOOTH[3]) / E
                total = done[c] * scale
                top = ((E + 0.5) * total - done[3 + c] * scale) * (1.0 / E)
                for p, part in ((0, total - top), (1, top)):
                    for j, weight in ((0, 1.0 - pb), (1, pb)):
                        row = jnp.sum(part * weight, axis=0, keepdims=True)
                        at = (p * 3 + c) * 8 + ey + j
                        ysum[pl.ds(at, 1), :] = ysum[pl.ds(at, 1), :] + row
        return 0

    lax.fori_loop(0, PER_ROW, element_row, 0)
    voxel = iota((NXY, NXY), 0)
    node = iota((NXY, NXY), 1)
    upper = ((voxel % E).astype(jnp.float32) + 0.5) / E
    to_nodes = jnp.where(voxel // E == node, 1.0 - upper, 0.0) + jnp.where(voxel // E + 1 == node, upper, 0.0)
    rhs_ref[...] = jnp.dot(
        ysum[...], to_nodes, preferred_element_type=jnp.float32, precision=lax.Precision.HIGHEST
    )


def layer_kernel(offs, lo, hi, vol_ref, tomo_ref, res_ref, rhs_ref, volf, xf, grads, lhs, win, ysum):
    filter_planes(tomo_ref, xf, grads)
    spread_volume(vol_ref, volf)

    def nodes(p, c, i):
        return (hi if p else lo)[c, i]

    warp_layer(offs, nodes, volf, tomo_ref, grads, lhs, win, ysum, res_ref, rhs_ref)


def layer(offsets, lo, hi, vol, tomo):
    smem = pl.BlockSpec(memory_space=pltpu.SMEM)
    vmem = pl.BlockSpec(memory_space=pltpu.VMEM)
    tall = E + 2 * RADIUS
    return pl.pallas_call(
        layer_kernel,
        out_shape=(
            jax.ShapeDtypeStruct((E, NXY, NXY), jnp.bfloat16),
            jax.ShapeDtypeStruct((48, NXY), jnp.float32),
        ),
        in_specs=[smem, smem, smem, vmem, vmem],
        out_specs=(vmem, vmem),
        scratch_shapes=[
            pltpu.VMEM((VPLANES, VROWS, NXY), jnp.float32),
            pltpu.VMEM((tall, NXY, 2 * NXY), jnp.bfloat16),
            pltpu.VMEM((3, tall, NXY, NXY), jnp.float32),
            pltpu.VMEM((WPLANES * WIN, PER_ROW * NXY), jnp.bfloat16),
            pltpu.VMEM((2, WPLANES * WIN, NXY), jnp.float32),
            pltpu.VMEM((48, NXY), jnp.float32),
        ],
        compiler_params=pltpu.CompilerParams(vmem_limit_bytes=48 << 20),
    )(offsets, lo, hi, vol, tomo)


def body(tomogram, deformed, subvoxel, offsets):
    ref_slab = lax.all_gather(tomogram, "scan", axis=0, tiled=True)
    extended = padded_2(ref_slab, "brick", 0, RADIUS)
    above = passed_along(subvoxel, "brick", -1)
    vol = padded_2(deformed[0], "brick", 0, HALO)
    residual, rhs = layer(offsets[0], subvoxel[0, :, 0], above[0, :, 0], vol, extended)
    rhs = rhs.reshape(2, 3, 8, NXY)[:, :, :NODES, :NODES].reshape(2, 1, 3, 1, NODES * NODES)
    node_rhs = rhs[0] + passed_along(rhs[1], "brick", 1)
    return residual[None], node_rhs


def solution(mesh):
    return jax.shard_map(
        body,
        mesh=mesh,
        in_specs=(
            P(("brick", "scan"), None, None),
            P("scan", "brick", None, None),
            P("scan", None, "brick", None),
            P("scan", None, "brick"),
        ),
        out_specs=(P("scan", "brick", None, None), P("scan", None, "brick", None)),
        check_vma=False,
    )
```

time: 361 us -> 86.2 us (0.24)
  the two profiles are of different devices: /device:TPU:70 before, /device:TPU:6 now
where the time goes in v1:
time: 86.2 us; the launch traced here: 85.9 us
  waiting for transfers between devices  25.5 us (30%)
  starting transfers between devices  23.6 us (27%)
  Pallas kernels  19.1 us (22%)
  between operations  14.2 us (16%)
  local copies, waits for them, and re-layouts  2.44 us (3%)
  other arithmetic  0.96 us (1%)
    pallas_call x1, Pallas kernels, layer(): pl.pallas_call(layer_kernel, out_shape=(jax.ShapeDtypeStruct((E, NXY, NXY...  19.1 us
    ppermute x2, waiting for transfers between devices, passed_along(): return lax.ppermute(block, axis, route)  14.3 us
    ppermute x2, starting transfers between devices, padded_2(): lax.ppermute(head, axis, [((i + 1) % count, i) for i in range(ends)])  12.7 us
    all_gather x1, waiting for transfers between devices, body(): ref_slab = lax.all_gather(tomogram, 'scan', axis=0, tiled=True)  8.46 us
    ppermute x2, starting transfers between devices, passed_along(): return lax.ppermute(block, axis, route)  5.44 us
    ppermute x2, starting transfers between devices, padded_2(): lax.ppermute(tail, axis, [(i, (i + 1) % count) for i in range(ends)])  5.41 us
    slice x2, local copies, waits for them, and re-layouts, padded_2(): lax.slice_in_dim(cells, cells.shape[dim] - width, cells.shape[dim], axis=...  2.25 us
  transfers between devices with their start and end apart: 7, of which 5 were waited for; matrix products, arithmetic and copies ran while one was open for 3% of the time, Pallas kernels for 0%

profile of v1, /device:TPU:6, one launch (start us, length us, event | category | flops | bytes accessed | tf_op | source)
XLA Modules:
  0.0 85.9 jit_solution(17504472452468770988)
XLA Ops:
  7.2 0.0 copy-start
  7.2 0.0 copy-start.3
  7.2 0.0 copy-start.2
  7.2 0.0 all-gather.2.cloned.1.call-start
  7.2 0.7 all-gather.2.cloned.1.call-update
  7.9 1.3 %slice_bitcast_fusion.1 = (bf16[16,128,128]{2,1,0:T(8,128)(2,1)S(1)}, bf16[16,128,128]{2,1,0:T(8,128)(2,1)S(1)}) fusion(bf16[1,32,128,128]{3,2,1,0:T(8,128)(2,1)} %param.5), kind=kLoop, calls=%fused_computation.3 | loop fusion | bytes 2097152 | tf_op jit(solution)/shard_map/slice | solution.py:46
  9.2 3.5 %collective-permute-start.1 = (bf16[16,128,128]{2,1,0:T(8,128)(2,1)S(1)}, bf16[16,128,128]{2,1,0:T(8,128)(2,1)S(1)}, u32[]{:S(2)}, u32[]{:S(2)}) collective-permute-start(bf16[16,128,128]{2,1,0:T(8,128)(2,1)S(1)} %get-tuple-element.14), channel_id=1, source_target_pairs={{0,4},{4,8},{8,12},{12,16},{16,20},{20,24},{24,28},{28,32},{32,36}... | collective-permute-start | bytes 1572872 | tf_op jit(solution)/shard_map/ppermute | solution.py:49
  12.7 5.4 %collective-permute-start.2 = (bf16[16,128,128]{2,1,0:T(8,128)(2,1)S(1)}, bf16[16,128,128]{2,1,0:T(8,128)(2,1)S(1)}, u32[]{:S(2)}, u32[]{:S(2)}) collective-permute-start(bf16[16,128,128]{2,1,0:T(8,128)(2,1)S(1)} %get-tuple-element.15), channel_id=1, source_target_pairs={{4,0},{8,4},{12,8},{16,12},{20,16},{24,20},{28,24},{32,28},{36,32}... | collective-permute-start | bytes 1572872 | tf_op jit(solution)/shard_map/ppermute | solution.py:51
  18.1 0.0 copy-done.3
  18.1 3.5 %collective-permute-start = (f32[1,3,1,25]{3,2,1,0:T(1,128)S(1)}, f32[1,3,1,25]{3,2,1,0:T(1,128)S(1)}, u32[]{:S(2)}, u32[]{:S(2)}) collective-permute-start(f32[1,3,1,25]{3,2,1,0:T(1,128)S(1)} %copy-done.3), channel_id=1, source_target_pairs={{4,0},{8,4},{12,8},{16,12},{20,16},{24,20},{28,24},{32,28},{36,32}... | collective-permute-start | bytes 908 | tf_op jit(solution)/shard_map/ppermute | solution.py:60
  21.7 0.0 copy-done.2
  21.7 7.3 %collective-permute-done = f32[1,3,1,25]{3,2,1,0:T(1,128)S(1)} collective-permute-done((f32[1,3,1,25]{3,2,1,0:T(1,128)S(1)}, f32[1,3,1,25]{3,2,1,0:T(1,128)S(1)}, u32[]{:S(2)}, u32[]{:S(2)}) %collective-permute-start) | collective-permute-done | bytes 332 | tf_op jit(solution)/shard_map/ppermute | solution.py:60
  29.0 8.5 %all-gather.2.cloned.1.call-done = bf16[32,128,128]{2,1,0:T(8,128)(2,1)} async-done(((bf16[8,128,128]{2,1,0:T(8,128)(2,1)}), bf16[32,128,128]{2,1,0:T(8,128)(2,1)}) %all-gather.2.cloned.1.call-update) | async-done | bytes 1048592 | tf_op jit(solution)/shard_map/all_gather | solution.py:280
  37.5 1.0 %fusion = (bf16[3,128,128]{2,1,0:T(8,128)(2,1)S(1)}, bf16[3,128,128]{2,1,0:T(8,128)(2,1)S(1)}) fusion(bf16[32,128,128]{2,1,0:T(8,128)(2,1)} %all-gather.2.cloned.1.call-done), kind=kLoop, calls=%fused_computation.10 | loop fusion | bytes 393216 | tf_op jit(solution)/shard_map/slice | solution.py:46
  38.4 1.9 %collective-permute-start.3 = (bf16[3,128,128]{2,1,0:T(8,128)(2,1)S(1)}, bf16[3,128,128]{2,1,0:T(8,128)(2,1)S(1)}, u32[]{:S(2)}, u32[]{:S(2)}) collective-permute-start(bf16[3,128,128]{2,1,0:T(8,128)(2,1)S(1)} %get-tuple-element.12), channel_id=1, source_target_pairs={{0,4},{4,8},{8,12},{12,16},{16,20},{20,24},{24,28},{28,32},{32,36}... | collective-permute-start | bytes 294920 | tf_op jit(solution)/shard_map/ppermute | solution.py:49
  40.4 7.4 %collective-permute-start.4 = (bf16[3,128,128]{2,1,0:T(8,128)(2,1)S(1)}, bf16[3,128,128]{2,1,0:T(8,128)(2,1)S(1)}, u32[]{:S(2)}, u32[]{:S(2)}) collective-permute-start(bf16[3,128,128]{2,1,0:T(8,128)(2,1)S(1)} %get-tuple-element.13), channel_id=1, source_target_pairs={{4,0},{8,4},{12,8},{16,12},{20,16},{24,20},{28,24},{32,28},{36,32}... | collective-permute-start | bytes 294920 | tf_op jit(solution)/shard_map/ppermute | solution.py:51
  47.7 0.0 collective-permute-done.1
  47.8 0.0 collective-permute-done.2
  47.8 0.0 copy-done
  47.8 0.0 copy-start.1
  47.8 0.2 pad_maximum_fusion.vol_ref
  48.0 1.0 %collective-permute-done.3 = bf16[3,128,128]{2,1,0:T(8,128)(2,1)S(1)} collective-permute-done((bf16[3,128,128]{2,1,0:T(8,128)(2,1)S(1)}, bf16[3,128,128]{2,1,0:T(8,128)(2,1)S(1)}, u32[]{:S(2)}, u32[]{:S(2)}) %collective-permute-start.3) | collective-permute-done | bytes 98336 | tf_op jit(solution)/shard_map/ppermute | solution.py:49
  49.0 1.2 %collective-permute-done.4 = bf16[3,128,128]{2,1,0:T(8,128)(2,1)S(1)} collective-permute-done((bf16[3,128,128]{2,1,0:T(8,128)(2,1)S(1)}, bf16[3,128,128]{2,1,0:T(8,128)(2,1)S(1)}, u32[]{:S(2)}, u32[]{:S(2)}) %collective-permute-start.4) | collective-permute-done | bytes 98336 | tf_op jit(solution)/shard_map/ppermute | solution.py:51
  50.2 0.0 copy-done.1
  50.2 0.2 pad_maximum_fusion.1.tomo_ref
  50.3 19.1 %shard_map.59 = (bf16[32,128,128]{2,1,0:T(8,128)(2,1)}, f32[48,128]{1,0:T(8,128)S(1)}) custom-call(s32[3,16]{1,0:T(4,128)S(1)} %bitcast.28, f32[3,25]{1,0:T(4,128)S(1)} %bitcast.27, f32[3,25]{1,0:T(4,128)S(1)} %bitcast.29, bf16[64,128,128]{2,1,0:T(8,128)(2,1)S(1)} %pad_maximum_fusion.vol_ref, bf16[38,128,128]{2,1,0:T(8,128)(2,1)S(1)} %pad_maximum_fusion.1.tomo_ref), custom_call_target="tpu_custom_call" | custom-call | tf_op jit(solution)/shard_map/pallas_call | solution.py:259
  69.4 0.1 squeeze.23
  69.5 1.9 %collective-permute-start.5 = (f32[1,3,1,25]{3,0,1,2:T(1,128)S(1)}, f32[1,3,1,25]{3,0,1,2:T(1,128)S(1)}, u32[]{:S(2)}, u32[]{:S(2)}) collective-permute-start(f32[1,3,1,25]{3,0,1,2:T(1,128)S(1)} %squeeze.23), channel_id=1, source_target_pairs={{0,4},{4,8},{8,12},{12,16},{16,20},{20,24},{24,28},{28,32},{32,36}... | collective-permute-start | bytes 908 | tf_op jit(solution)/shard_map/ppermute | solution.py:60
  71.4 0.1 squeeze.22
  71.5 6.9 %collective-permute-done.5 = f32[1,3,1,25]{3,0,1,2:T(1,128)S(1)} collective-permute-done((f32[1,3,1,25]{3,0,1,2:T(1,128)S(1)}, f32[1,3,1,25]{3,0,1,2:T(1,128)S(1)}, u32[]{:S(2)}, u32[]{:S(2)}) %collective-permute-start.5) | collective-permute-done | bytes 332 | tf_op jit(solution)/shard_map/ppermute | solution.py:60
  78.5 0.6 add_bitcast_fusion
  (4 shorter events, 0.0 us)
Async XLA Ops:
  7.2 40.6 %copy-start = (bf16[1,32,128,128]{3,2,1,0:T(8,128)(2,1)S(1)}, bf16[1,32,128,128]{3,2,1,0:T(8,128)(2,1)}, u32[]{:S(2)}) copy-start(bf16[1,32,128,128]{3,2,1,0:T(8,128)(2,1)} %param.5) | copy-start | bytes 3145732
  7.2 10.9 %copy-start.3 = (f32[1,3,1,25]{3,2,1,0:T(1,128)S(1)}, f32[1,3,1,25]{3,2,1,0:T(1,128)}, u32[]{:S(2)}) copy-start(f32[1,3,1,25]{3,2,1,0:T(1,128)} %param.6) | copy-start | bytes 904
  7.2 14.5 %copy-start.2 = (s32[1,3,16]{2,0,1:T(1,128)S(1)}, s32[1,3,16]{2,0,1:T(1,128)}, u32[]{:S(2)}) copy-start(s32[1,3,16]{2,0,1:T(1,128)} %param.7) | copy-start | bytes 580
  7.2 30.3 %all-gather.2.cloned.1.call-start = ((), (), s32[]{:S(2)}) async-start(), calls=%async_computation | async-start | bytes 1310720 | tf_op jit(solution)/shard_map/all_gather | solution.py:280
  9.2 38.5 %collective-permute-start.1 = (bf16[16,128,128]{2,1,0:T(8,128)(2,1)S(1)}, bf16[16,128,128]{2,1,0:T(8,128)(2,1)S(1)}, u32[]{:S(2)}, u32[]{:S(2)}) collective-permute-start(bf16[16,128,128]{2,1,0:T(8,128)(2,1)S(1)} %get-tuple-element.14), channel_id=1, source_target_pairs={{0,4},{4,8},{8,12},{12,16},{16,20},{20,24},{24,28},{28,32},{32,36}... | collective-permute-start | bytes 1572872 | tf_op jit(solution)/shard_map/ppermute | solution.py:49
  12.7 35.0 %collective-permute-start.2 = (bf16[16,128,128]{2,1,0:T(8,128)(2,1)S(1)}, bf16[16,128,128]{2,1,0:T(8,128)(2,1)S(1)}, u32[]{:S(2)}, u32[]{:S(2)}) collective-permute-start(bf16[16,128,128]{2,1,0:T(8,128)(2,1)S(1)} %get-tuple-element.15), channel_id=1, source_target_pairs={{4,0},{8,4},{12,8},{16,12},{20,16},{24,20},{28,24},{32,28},{36,32}... | collective-permute-start | bytes 1572872 | tf_op jit(solution)/shard_map/ppermute | solution.py:51
  18.1 10.9 %collective-permute-start = (f32[1,3,1,25]{3,2,1,0:T(1,128)S(1)}, f32[1,3,1,25]{3,2,1,0:T(1,128)S(1)}, u32[]{:S(2)}, u32[]{:S(2)}) collective-permute-start(f32[1,3,1,25]{3,2,1,0:T(1,128)S(1)} %copy-done.3), channel_id=1, source_target_pairs={{4,0},{8,4},{12,8},{16,12},{20,16},{24,20},{28,24},{32,28},{36,32}... | collective-permute-start | bytes 908 | tf_op jit(solution)/shard_map/ppermute | solution.py:60
  38.4 10.6 %collective-permute-start.3 = (bf16[3,128,128]{2,1,0:T(8,128)(2,1)S(1)}, bf16[3,128,128]{2,1,0:T(8,128)(2,1)S(1)}, u32[]{:S(2)}, u32[]{:S(2)}) collective-permute-start(bf16[3,128,128]{2,1,0:T(8,128)(2,1)S(1)} %get-tuple-element.12), channel_id=1, source_target_pairs={{0,4},{4,8},{8,12},{12,16},{16,20},{20,24},{24,28},{28,32},{32,36}... | collective-permute-start | bytes 294920 | tf_op jit(solution)/shard_map/ppermute | solution.py:49
  40.4 9.8 %collective-permute-start.4 = (bf16[3,128,128]{2,1,0:T(8,128)(2,1)S(1)}, bf16[3,128,128]{2,1,0:T(8,128)(2,1)S(1)}, u32[]{:S(2)}, u32[]{:S(2)}) collective-permute-start(bf16[3,128,128]{2,1,0:T(8,128)(2,1)S(1)} %get-tuple-element.13), channel_id=1, source_target_pairs={{4,0},{8,4},{12,8},{16,12},{20,16},{24,20},{28,24},{32,28},{36,32}... | collective-permute-start | bytes 294920 | tf_op jit(solution)/shard_map/ppermute | solution.py:51
  47.8 2.4 %copy-start.1 = (bf16[32,128,128]{2,1,0:T(8,128)(2,1)S(1)}, bf16[32,128,128]{2,1,0:T(8,128)(2,1)}, u32[]{:S(2)}) copy-start(bf16[32,128,128]{2,1,0:T(8,128)(2,1)} %all-gather.2.cloned.1.call-done) | copy-start | bytes 3145732
  69.5 8.9 %collective-permute-start.5 = (f32[1,3,1,25]{3,0,1,2:T(1,128)S(1)}, f32[1,3,1,25]{3,0,1,2:T(1,128)S(1)}, u32[]{:S(2)}, u32[]{:S(2)}) collective-permute-start(f32[1,3,1,25]{3,0,1,2:T(1,128)S(1)} %squeeze.23), channel_id=1, source_target_pairs={{0,4},{4,8},{8,12},{12,16},{16,20},{20,24},{24,28},{28,32},{32,36}... | collective-permute-start | bytes 908 | tf_op jit(solution)/shard_map/ppermute | solution.py:60
Sparse Core Ops, SparseCore 0:
  9.7 27.7 all-gather.1

commit v2 on v1

--- a/solution.py
+++ b/solution.py
@@ -1,5 +1,3 @@
-import functools
-
 import jax
 import jax.numpy as jnp
 import ml_dtypes
@@ -39,27 +37,6 @@
 SMOOTH, SLOPE = filter_taps()
 
 
-def padded_2(cells, axis, dim, width):
-    count = lax.axis_size(axis)
-    ends = count - 1
-    head = lax.slice_in_dim(cells, 0, width, axis=dim)
-    tail = lax.slice_in_dim(cells, cells.shape[dim] - width, cells.shape[dim], axis=dim)
-    return jnp.concatenate(
-        [
-            lax.ppermute(tail, axis, [(i, (i + 1) % count) for i in range(ends)]),
-            cells,
-            lax.ppermute(head, axis, [((i + 1) % count, i) for i in range(ends)]),
-        ],
-        axis=dim,
-    )
-
-
-def passed_along(block, axis, distance):
-    devices = range(lax.axis_size(axis))
-    route = [(i - distance, i) for i in devices if i - distance in devices]
-    return lax.ppermute(block, axis, route)
-
-
 def iota(shape, dim):
     return lax.broadcasted_iota(jnp.int32, shape, dim)
 
@@ -69,13 +46,6 @@
     for tap in range(2 * RADIUS + 1):
         table = jnp.where(distance == tap - RADIUS, taps[tap], table)
     return table
-
-
-def hat(shape, dim, node):
-    voxel = iota(shape, dim)
-    elem = voxel // E
-    upper = ((voxel % E).astype(jnp.float32) + 0.5) / E
-    return jnp.where(elem == node, 1.0 - upper, jnp.where(elem + 1 == node, upper, 0.0))
 
 
 def filter_planes(tomo_ref, xf, grads):
@@ -104,20 +74,7 @@
     lax.fori_loop(0, pairs, y_step, 0)
 
 
-def spread_volume(vol_ref, volf):
-    zeros_lo = jnp.zeros((YPAD, NXY), jnp.float32)
-    zeros_hi = jnp.zeros((VROWS - YPAD - NXY, NXY), jnp.float32)
-
-    def step(z, _):
-        volf[z, :YPAD] = zeros_lo
-        volf[z, YPAD : YPAD + NXY] = vol_ref[z].astype(jnp.float32)
-        volf[z, YPAD + NXY :] = zeros_hi
-        return 0
-
-    lax.fori_loop(0, VPLANES, step, 0)
-
-
-def warp_layer(offs, nodes, volf, tomo_ref, grads, lhs, win, ysum, res_ref, rhs_ref):
+def warp_layer(offs, fields, volf, tomo_ref, grads, lhs, win, ysum, res_ref, row_done):
     ysum[...] = jnp.zeros_like(ysum)
 
     def element_row(ey, _):
@@ -159,12 +116,9 @@
             for c in range(3):
                 planes = []
                 for p in range(2):
-                    lo = jnp.zeros((16, NXY), jnp.float32)
-                    hi = jnp.zeros((16, NXY), jnp.float32)
-                    for ix in range(NODES):
-                        weight = hat((16, NXY), 1, ix)
-                        lo = lo + nodes(p, c, ey * NODES + ix) * weight
-                        hi = hi + nodes(p, c, (ey + 1) * NODES + ix) * weight
+                    at = p * 8 + c
+                    lo = fields[ey, at : at + 1, :]
+                    hi = fields[ey + 1, at : at + 1, :]
                     planes.append(lo * (1.0 - pb) + hi * pb)
                 rise = (planes[1] - planes[0]) * (1.0 / E)
                 start.append(planes[0] + 0.5 * rise)
@@ -228,62 +182,350 @@
                 for p, part in ((0, total - top), (1, top)):
                     for j, weight in ((0, 1.0 - pb), (1, pb)):
                         row = jnp.sum(part * weight, axis=0, keepdims=True)
-                        at = (p * 3 + c) * 8 + ey + j
-                        ysum[pl.ds(at, 1), :] = ysum[pl.ds(at, 1), :] + row
+                        at = p * 8 + c
+                        ysum[ey + j, at : at + 1, :] = ysum[ey + j, at : at + 1, :] + row
+        row_done(ey)
         return 0
 
     lax.fori_loop(0, PER_ROW, element_row, 0)
+
+
+def node_lanes(iy):
+    node = iota((NXY, NXY), 1) - NODES * iy
     voxel = iota((NXY, NXY), 0)
-    node = iota((NXY, NXY), 1)
     upper = ((voxel % E).astype(jnp.float32) + 0.5) / E
-    to_nodes = jnp.where(voxel // E == node, 1.0 - upper, 0.0) + jnp.where(voxel // E + 1 == node, upper, 0.0)
-    rhs_ref[...] = jnp.dot(
-        ysum[...], to_nodes, preferred_element_type=jnp.float32, precision=lax.Precision.HIGHEST
-    )
-
-
-def layer_kernel(offs, lo, hi, vol_ref, tomo_ref, res_ref, rhs_ref, volf, xf, grads, lhs, win, ysum):
-    filter_planes(tomo_ref, xf, grads)
-    spread_volume(vol_ref, volf)
-
-    def nodes(p, c, i):
-        return (hi if p else lo)[c, i]
-
-    warp_layer(offs, nodes, volf, tomo_ref, grads, lhs, win, ysum, res_ref, rhs_ref)
-
-
-def layer(offsets, lo, hi, vol, tomo):
+    weight = jnp.where(voxel // E == node, 1.0 - upper, 0.0) + jnp.where(voxel // E + 1 == node, upper, 0.0)
+    return jnp.where(node < NODES, weight, 0.0)
+
+
+def node_fields(nodes, fields):
+    for iy in range(NODES):
+        fields[iy] = lax.dot_general(
+            nodes[...],
+            node_lanes(iy),
+            (((1,), (1,)), ((), ())),
+            preferred_element_type=jnp.float32,
+            precision=lax.Precision.HIGHEST,
+        )
+
+
+def node_sums(ysum):
+    total = jnp.zeros((16, NXY), jnp.float32)
+    for iy in range(NODES):
+        total = total + jnp.dot(
+            ysum[iy], node_lanes(iy), preferred_element_type=jnp.float32, precision=lax.Precision.HIGHEST
+        )
+    return total
+
+
+UP, DOWN, SIBLING, OTHER, RELAY, LOW_A, LOW_B, LOW_RELAY, HIGH_A, HIGH_B, HIGH_RELAY, NODE, TAIL = range(13)
+
+
+def step_kernel(
+    offs, sub_ref, tomo_hbm, vol_hbm, res_hbm, rhs_ref,
+    own, halo, tomo, volf, xf, grads, lhs, win, ysum, fields, nodes, above, res, sums, tail,
+    send, recv, local,
+):
+    bricks = lax.axis_size("brick")
+    b = lax.axis_index("brick")
+    s = lax.axis_index("scan")
+    block = tomo_hbm.shape[0]
+    has_above = b < bricks - 1
+    has_below = b > 0
+    odd = lax.rem(s, 2) == 1
+    sibling = s + 1 - 2 * lax.rem(s, 2)
+    other = lax.rem(s + 2, 4)
+
+    def remote(kind, src, dst, brick, scan):
+        return pltpu.make_async_remote_copy(
+            src_ref=src,
+            dst_ref=dst,
+            send_sem=send.at[kind],
+            recv_sem=recv.at[kind],
+            device_id={"brick": brick, "scan": scan},
+            device_id_type=pl.DeviceIdType.MESH,
+        )
+
+    def block_at(i):
+        return tomo.at[pl.ds(RADIUS + block * i, block)]
+
+    low_edge = tomo.at[pl.ds(0, RADIUS)]
+    high_edge = tomo.at[pl.ds(RADIUS + E, RADIUS)]
+    up = remote(UP, vol_hbm.at[0, pl.ds(E - HALO, HALO)], halo.at[0], b + 1, s)
+    down = remote(DOWN, vol_hbm.at[0, pl.ds(0, HALO)], halo.at[1], b - 1, s)
+    to_sibling = remote(SIBLING, tomo_hbm, block_at(s), b, sibling)
+    to_other = remote(OTHER, tomo_hbm, block_at(s), b, other)
+    relay = remote(RELAY, block_at(other), block_at(other), b, sibling)
+    from_relay = remote(RELAY, block_at(lax.rem(sibling + 2, 4)), block_at(lax.rem(sibling + 2, 4)), b, sibling)
+    from_sibling = remote(SIBLING, tomo_hbm, block_at(sibling), b, sibling)
+    from_other = remote(OTHER, tomo_hbm, block_at(other), b, other)
+    last_planes = tomo_hbm.at[pl.ds(block - RADIUS, RADIUS)]
+    first_planes = tomo_hbm.at[pl.ds(0, RADIUS)]
+    low_a = remote(LOW_A, last_planes, low_edge, b + 1, 3)
+    low_b = remote(LOW_B, last_planes, low_edge, b + 1, 1)
+    low_relay = remote(LOW_RELAY, low_edge, low_edge, b, sibling)
+    high_a = remote(HIGH_A, first_planes, high_edge, b - 1, 0)
+    high_b = remote(HIGH_B, first_planes, high_edge, b - 1, 2)
+    high_relay = remote(HIGH_RELAY, high_edge, high_edge, b, sibling)
+    node = remote(NODE, sub_ref, above, b - 1, s)
+
+    get_own = pltpu.make_async_copy(vol_hbm.at[0], own, local.at[0])
+    get_tomo = pltpu.make_async_copy(tomo_hbm, block_at(s), local.at[1])
+    get_own.start()
+    get_tomo.start()
+
+    barrier = pltpu.get_barrier_semaphore()
+
+    def greet(brick, scan):
+        pl.semaphore_signal(
+            barrier, inc=1, device_id={"brick": brick, "scan": scan}, device_id_type=pl.DeviceIdType.MESH
+        )
+
+    greet(b, sibling)
+    greet(b, other)
+
+    @pl.when(has_above)
+    def _():
+        greet(b + 1, s)
+
+        @pl.when(s == 3)
+        def _():
+            greet(b + 1, 1)
+
+        @pl.when(s == 2)
+        def _():
+            greet(b + 1, 0)
+
+    @pl.when(has_below)
+    def _():
+        greet(b - 1, s)
+
+        @pl.when(s == 1)
+        def _():
+            greet(b - 1, 3)
+
+        @pl.when(s == 0)
+        def _():
+            greet(b - 1, 2)
+
+    from_above = jnp.where(has_above, jnp.where(s >= 2, 2, 1), 0)
+    from_below = jnp.where(has_below, jnp.where(s <= 1, 2, 1), 0)
+    pl.semaphore_wait(barrier, 2 + from_above + from_below)
+
+    to_other.start()
+    to_sibling.start()
+
+    @pl.when(has_above & (s == 3))
+    def _():
+        low_a.start()
+        low_b.start()
+
+    @pl.when(has_below & (s == 0))
+    def _():
+        high_a.start()
+        high_b.start()
+
+    @pl.when(has_above)
+    def _():
+        up.start()
+
+    @pl.when(has_below)
+    def _():
+        down.start()
+        node.start()
+
+    zeros_lo = jnp.zeros((YPAD, NXY), jnp.float32)
+    zeros_hi = jnp.zeros((VROWS - YPAD - NXY, NXY), jnp.float32)
+
+    def borders(z, _):
+        volf[z, :YPAD] = zeros_lo
+        volf[z, YPAD + NXY :] = zeros_hi
+        return 0
+
+    lax.fori_loop(0, VPLANES, borders, 0)
+    nodes[...] = jnp.zeros_like(nodes)
+    for c in range(3):
+        nodes[c : c + 1, : NODES * NODES] = sub_ref[0, c]
+
+    @pl.when(jnp.logical_not(has_below))
+    def _():
+        halo[0] = jnp.zeros((HALO, NXY, NXY), jnp.bfloat16)
+        tomo[:RADIUS] = jnp.zeros((RADIUS, NXY, NXY), jnp.bfloat16)
+
+    @pl.when(jnp.logical_not(has_above))
+    def _():
+        halo[1] = jnp.zeros((HALO, NXY, NXY), jnp.bfloat16)
+        tomo[RADIUS + E :] = jnp.zeros((RADIUS, NXY, NXY), jnp.bfloat16)
+
+    get_own.wait()
+
+    def spread_own(z, _):
+        volf[HALO + z, YPAD : YPAD + NXY] = own[z].astype(jnp.float32)
+        return 0
+
+    lax.fori_loop(0, E, spread_own, 0)
+
+    from_other.wait_recv()
+    relay.start()
+
+    @pl.when(has_below & odd)
+    def _():
+        @pl.when(s == 3)
+        def _():
+            low_a.wait_recv()
+
+        @pl.when(s == 1)
+        def _():
+            low_b.wait_recv()
+
+        low_relay.start()
+
+    @pl.when(has_above & jnp.logical_not(odd))
+    def _():
+        @pl.when(s == 0)
+        def _():
+            high_a.wait_recv()
+
+        @pl.when(s == 2)
+        def _():
+            high_b.wait_recv()
+
+        high_relay.start()
+
+    get_tomo.wait()
+    from_sibling.wait_recv()
+    from_relay.wait_recv()
+
+    @pl.when(has_below & jnp.logical_not(odd))
+    def _():
+        low_relay.wait_recv()
+
+    @pl.when(has_above & odd)
+    def _():
+        high_relay.wait_recv()
+
+    filter_planes(tomo, xf, grads)
+
+    @pl.when(has_above)
+    def _():
+        node.wait_recv()
+        for c in range(3):
+            nodes[8 + c : 9 + c, : NODES * NODES] = above[0, c]
+        down.wait_recv()
+
+    @pl.when(has_below)
+    def _():
+        up.wait_recv()
+
+    node_fields(nodes, fields)
+
+    def spread_halo(z, _):
+        volf[z, YPAD : YPAD + NXY] = halo[0, z].astype(jnp.float32)
+        volf[HALO + E + z, YPAD : YPAD + NXY] = halo[1, z].astype(jnp.float32)
+        return 0
+
+    lax.fori_loop(0, HALO, spread_halo, 0)
+
+    def put_row(ey):
+        rows = pl.ds(pl.multiple_of(ey * E, E), E)
+        return pltpu.make_async_copy(res.at[:, rows], res_hbm.at[:, rows], local.at[2 + ey])
+
+    warp_layer(offs, fields, volf, tomo, grads, lhs, win, ysum, res, lambda ey: put_row(ey).start())
+    sums[...] = node_sums(ysum)
+    to_above = remote(TAIL, sums.at[pl.ds(8, 8)], tail, b + 1, s)
+
+    @pl.when(has_above)
+    def _():
+        to_above.start()
+
+    to_other.wait_send()
+    to_sibling.wait_send()
+    relay.wait_send()
+
+    @pl.when(has_above & (s == 3))
+    def _():
+        low_a.wait_send()
+        low_b.wait_send()
+
+    @pl.when(has_below & (s == 0))
+    def _():
+        high_a.wait_send()
+        high_b.wait_send()
+
+    @pl.when(has_below & odd)
+    def _():
+        low_relay.wait_send()
+
+    @pl.when(has_above & jnp.logical_not(odd))
+    def _():
+        high_relay.wait_send()
+
+    @pl.when(has_above)
+    def _():
+        up.wait_send()
+
+    @pl.when(has_below)
+    def _():
+        down.wait_send()
+        node.wait_send()
+
+    for ey in range(PER_ROW):
+        put_row(ey).wait()
+
+    @pl.when(jnp.logical_not(has_below))
+    def _():
+        tail[...] = jnp.zeros_like(tail)
+
+    @pl.when(has_below)
+    def _():
+        to_above.wait_recv()
+
+    final = sums[:8] + tail[...]
+    for c in range(3):
+        rhs_ref[0, c] = final[c : c + 1, : NODES * NODES]
+
+    @pl.when(has_above)
+    def _():
+        to_above.wait_send()
+
+
+def body(tomogram, deformed, subvoxel, offsets):
+    tall = E + 2 * RADIUS
     smem = pl.BlockSpec(memory_space=pltpu.SMEM)
     vmem = pl.BlockSpec(memory_space=pltpu.VMEM)
-    tall = E + 2 * RADIUS
-    return pl.pallas_call(
-        layer_kernel,
+    hbm = pl.BlockSpec(memory_space=pl.ANY)
+    residual, node_rhs = pl.pallas_call(
+        step_kernel,
         out_shape=(
             jax.ShapeDtypeStruct((E, NXY, NXY), jnp.bfloat16),
-            jax.ShapeDtypeStruct((48, NXY), jnp.float32),
+            jax.ShapeDtypeStruct(subvoxel.shape, jnp.float32),
         ),
-        in_specs=[smem, smem, smem, vmem, vmem],
-        out_specs=(vmem, vmem),
+        in_specs=[smem, vmem, hbm, hbm],
+        out_specs=(hbm, vmem),
         scratch_shapes=[
+            pltpu.VMEM((E, NXY, NXY), jnp.bfloat16),
+            pltpu.VMEM((2, HALO, NXY, NXY), jnp.bfloat16),
+            pltpu.VMEM((tall, NXY, NXY), jnp.bfloat16),
             pltpu.VMEM((VPLANES, VROWS, NXY), jnp.float32),
             pltpu.VMEM((tall, NXY, 2 * NXY), jnp.bfloat16),
             pltpu.VMEM((3, tall, NXY, NXY), jnp.float32),
             pltpu.VMEM((WPLANES * WIN, PER_ROW * NXY), jnp.bfloat16),
             pltpu.VMEM((2, WPLANES * WIN, NXY), jnp.float32),
-            pltpu.VMEM((48, NXY), jnp.float32),
+            pltpu.VMEM((NODES, 16, NXY), jnp.float32),
+            pltpu.VMEM((NODES, 16, NXY), jnp.float32),
+            pltpu.VMEM((16, NXY), jnp.float32),
+            pltpu.VMEM(subvoxel.shape, jnp.float32),
+            pltpu.VMEM((E, NXY, NXY), jnp.bfloat16),
+            pltpu.VMEM((16, NXY), jnp.float32),
+            pltpu.VMEM((8, NXY), jnp.float32),
+            pltpu.SemaphoreType.DMA((13,)),
+            pltpu.SemaphoreType.DMA((13,)),
+            pltpu.SemaphoreType.DMA((2 + PER_ROW,)),
         ],
-        compiler_params=pltpu.CompilerParams(vmem_limit_bytes=48 << 20),
-    )(offsets, lo, hi, vol, tomo)
-
-
-def body(tomogram, deformed, subvoxel, offsets):
-    ref_slab = lax.all_gather(tomogram, "scan", axis=0, tiled=True)
-    extended = padded_2(ref_slab, "brick", 0, RADIUS)
-    above = passed_along(subvoxel, "brick", -1)
-    vol = padded_2(deformed[0], "brick", 0, HALO)
-    residual, rhs = layer(offsets[0], subvoxel[0, :, 0], above[0, :, 0], vol, extended)
-    rhs = rhs.reshape(2, 3, 8, NXY)[:, :, :NODES, :NODES].reshape(2, 1, 3, 1, NODES * NODES)
-    node_rhs = rhs[0] + passed_along(rhs[1], "brick", 1)
+        compiler_params=pltpu.CompilerParams(
+            collective_id=0, has_side_effects=True, vmem_limit_bytes=48 << 20
+        ),
+    )(offsets[0], subvoxel, tomogram, deformed)
     return residual[None], node_rhs
 
 

time: 86.2 us -> 54.5 us (0.63)
  the two profiles are of different devices: /device:TPU:6 before, /device:TPU:7 now
where the time goes in v2:
time: 54.5 us; the launch traced here: 54.3 us
  Pallas kernels  48.6 us (89%)
  local copies, waits for them, and re-layouts  5.07 us (9%)
  between operations  0.64 us (1%)
    pallas_call x1, Pallas kernels, body(): pl.pallas_call(step_kernel, out_shape=(jax.ShapeDtypeStruct((E, NXY, NXY)...  48.6 us
    unnamed x9, local copies, waits for them, and re-layouts  5.07 us

profile of v2, /device:TPU:7, one launch (start us, length us, event | category | flops | bytes accessed | tf_op | source)
XLA Modules:
  0.0 54.3 jit_solution(13598715137109722338)
XLA Ops:
  0.6 0.7 %copy.8 = s32[1,3,16]{2,1,0:T(4,128)S(1)} copy(s32[1,3,16]{2,0,1:T(1,128)} %param.7) | data formatting | bytes 384
  1.3 0.0 copy-start.2
  1.3 0.7 %copy-done.2 = f32[1,3,1,25]{3,2,1,0:T(1,128)S(1)} copy-done((f32[1,3,1,25]{3,2,1,0:T(1,128)S(1)}, f32[1,3,1,25]{3,2,1,0:T(1,128)}, u32[]{:S(2)}) %copy-start.2) | copy-done | bytes 324
  2.0 0.0 copy-start
  2.0 1.2 %copy-done = bf16[1,32,128,128]{3,2,1,0:T(8,128)(2,1)S(1)} copy-done((bf16[1,32,128,128]{3,2,1,0:T(8,128)(2,1)S(1)}, bf16[1,32,128,128]{3,2,1,0:T(8,128)(2,1)}, u32[]{:S(2)}) %copy-start) | copy-done | bytes 1048600
  3.2 0.0 copy-start.1
  3.2 0.9 %copy-done.1 = bf16[8,128,128]{2,1,0:T(8,128)(2,1)S(1)} copy-done((bf16[8,128,128]{2,1,0:T(8,128)(2,1)S(1)}, bf16[8,128,128]{2,1,0:T(8,128)(2,1)}, u32[]{:S(2)}) %copy-start.1) | copy-done | bytes 262168
  4.2 48.6 %shard_map.59 = (bf16[32,128,128]{2,1,0:T(8,128)(2,1)S(1)}, f32[1,3,1,25]{3,2,1,0:T(1,128)S(1)}) custom-call(s32[3,16]{1,0:T(4,128)S(1)} %bitcast.5, f32[1,3,1,25]{3,2,1,0:T(1,128)S(1)} %copy-done.2, bf16[8,128,128]{2,1,0:T(8,128)(2,1)S(1)} %copy-done.1, bf16[1,32,128,128]{3,2,1,0:T(8,128)(2,1)S(1)} %copy-done), custom_call_target="tpu_custom_call" | custom-call | tf_op jit(solution)/shard_map/pallas_call | solution.py:497
  52.8 1.0 %copy.11 = bf16[1,32,128,128]{3,2,1,0:T(8,128)(2,1)} copy(bf16[1,32,128,128]{3,2,1,0:T(8,128)(2,1)S(1)} %bitcast.4) | data formatting | bytes 2097152
  53.7 0.6 %copy.12 = f32[1,3,1,25]{3,2,1,0:T(1,128)} copy(f32[1,3,1,25]{3,2,1,0:T(1,128)S(1)} %get-tuple-element.9) | data formatting | bytes 600
Async XLA Ops:
  1.3 0.7 %copy-start.2 = (f32[1,3,1,25]{3,2,1,0:T(1,128)S(1)}, f32[1,3,1,25]{3,2,1,0:T(1,128)}, u32[]{:S(2)}) copy-start(f32[1,3,1,25]{3,2,1,0:T(1,128)} %sub_ref.1) | copy-start | bytes 904
  2.0 1.2 %copy-start = (bf16[1,32,128,128]{3,2,1,0:T(8,128)(2,1)S(1)}, bf16[1,32,128,128]{3,2,1,0:T(8,128)(2,1)}, u32[]{:S(2)}) copy-start(bf16[1,32,128,128]{3,2,1,0:T(8,128)(2,1)} %vol_hbm.1) | copy-start | bytes 3145732
  3.2 0.9 %copy-start.1 = (bf16[8,128,128]{2,1,0:T(8,128)(2,1)S(1)}, bf16[8,128,128]{2,1,0:T(8,128)(2,1)}, u32[]{:S(2)}) copy-start(bf16[8,128,128]{2,1,0:T(8,128)(2,1)} %tomo_hbm.1) | copy-start | bytes 786436

commit v3 on v2

--- a/solution.py
+++ b/solution.py
@@ -48,51 +48,49 @@
     return table
 
 
-def filter_planes(tomo_ref, xf, grads):
+def write_bands(band_x, band_y):
     d = iota((NXY, NXY), 0) - iota((NXY, NXY), 1)
-    along_x = jnp.concatenate([band(d, SMOOTH), band(d, SLOPE)], axis=1).astype(jnp.bfloat16)
-    along_y = jnp.concatenate([band(-d, SMOOTH), band(-d, SLOPE)], axis=0).astype(jnp.bfloat16)
-    pairs = (E + 2 * RADIUS) // 2
-
-    def x_step(i, _):
-        two = tomo_ref[pl.ds(2 * i, 2)].reshape(2 * NXY, NXY)
-        out = jnp.dot(two, along_x, preferred_element_type=jnp.float32)
-        xf[pl.ds(2 * i, 2)] = out.astype(jnp.bfloat16).reshape(2, NXY, 2 * NXY)
-        return 0
-
-    lax.fori_loop(0, pairs, x_step, 0)
-
-    def y_step(i, _):
-        for k in range(2):
-            z = 2 * i + k
-            out = jnp.dot(along_y, xf[z], preferred_element_type=jnp.float32)
-            grads[0, z] = out[:NXY, :NXY]
-            grads[1, z] = out[NXY:, :NXY]
-            grads[2, z] = out[:NXY, NXY:]
-        return 0
-
-    lax.fori_loop(0, pairs, y_step, 0)
-
-
-def warp_layer(offs, fields, volf, tomo_ref, grads, lhs, win, ysum, res_ref, row_done):
-    ysum[...] = jnp.zeros_like(ysum)
-
+    band_x[...] = jnp.concatenate([band(d, SMOOTH), band(d, SLOPE)], axis=1).astype(jnp.bfloat16)
+    band_y[...] = jnp.concatenate([band(-d, SMOOTH), band(-d, SLOPE)], axis=0).astype(jnp.bfloat16)
+
+
+def filter_planes(band_x, band_y, tomo, grads, start, count):
+    planes = tomo[pl.ds(start, count)].reshape(count * NXY, NXY)
+    along_x = jnp.dot(planes, band_x[...], preferred_element_type=jnp.float32).astype(jnp.bfloat16)
+    for k in range(count):
+        out = jnp.dot(
+            band_y[...], along_x[k * NXY : (k + 1) * NXY], preferred_element_type=jnp.float32
+        )
+        grads[0, start + k] = out[:NXY, :NXY]
+        grads[1, start + k] = out[NXY:, :NXY]
+        grads[2, start + k] = out[:NXY, NXY:]
+
+
+def write_shifts(offs, shifts):
     def element_row(ey, _):
         src = iota((NXY, NXY), 0)
         dst = iota((NXY, NXY), 1)
-        blocks = []
         for ex in range(PER_ROW):
-            ox = offs[2, ey * PER_ROW + ex]
+            ox = offs[2, 0, ey * PER_ROW + ex]
             mine = dst // E == ex
             here = jnp.where(mine & (src == dst + ox), 1.0, 0.0)
             after = jnp.where(mine & (src == dst + ox + 1), 1.0, 0.0)
-            blocks.append(jnp.concatenate([here, after - here], axis=1))
-        shift = jnp.concatenate(blocks, axis=0).astype(jnp.bfloat16)
-
+            shifts[ey, ex * NXY : (ex + 1) * NXY, :] = jnp.concatenate(
+                [here, after - here], axis=1
+            ).astype(jnp.bfloat16)
+        return 0
+
+    lax.fori_loop(0, PER_ROW, element_row, 0)
+
+
+def warp_layer(offs, shifts, fields, volf, tomo_ref, grads, lhs, win, ysum, res_ref, row_done):
+    ysum[...] = jnp.zeros_like(ysum)
+
+    def element_row(ey, _):
         def gather_planes(q, _):
             for ex in range(PER_ROW):
-                oz = offs[0, ey * PER_ROW + ex] + HALO
-                oy = offs[1, ey * PER_ROW + ex] + ey * E + YPAD
+                oz = offs[0, 0, ey * PER_ROW + ex] + HALO
+                oy = offs[1, 0, ey * PER_ROW + ex] + ey * E + YPAD
                 two = []
                 for k in range(2):
                     z = jnp.minimum(2 * q + k + oz, VPLANES - 1)
@@ -106,7 +104,7 @@
         rows = WPLANES * WIN
         for r0 in range(0, rows, 480):
             r1 = min(r0 + 480, rows)
-            out = jnp.dot(lhs[r0:r1, :], shift, preferred_element_type=jnp.float32)
+            out = jnp.dot(lhs[r0:r1, :], shifts[ey], preferred_element_type=jnp.float32)
             win[0, r0:r1, :] = out[:, :NXY]
             win[1, r0:r1, :] = out[:, NXY:]
 
@@ -222,8 +220,8 @@
 
 
 def step_kernel(
-    offs, sub_ref, tomo_hbm, vol_hbm, res_hbm, rhs_ref,
-    own, halo, tomo, volf, xf, grads, lhs, win, ysum, fields, nodes, above, res, sums, tail,
+    offs, sub_hbm, tomo_hbm, vol_hbm, res_hbm, rhs_ref,
+    own, halo, tomo, res, volf, band_x, band_y, shifts, grads, lhs, win, ysum, fields, nodes, mine, above, sums, tail,
     send, recv, local,
 ):
     bricks = lax.axis_size("brick")
@@ -251,7 +249,7 @@
 
     low_edge = tomo.at[pl.ds(0, RADIUS)]
     high_edge = tomo.at[pl.ds(RADIUS + E, RADIUS)]
-    up = remote(UP, vol_hbm.at[0, pl.ds(E - HALO, HALO)], halo.at[0], b + 1, s)
+    up = remote(UP, vol_hbm.at[0, pl.ds(E - HALO + 1, HALO - 1)], halo.at[0, pl.ds(1, HALO - 1)], b + 1, s)
     down = remote(DOWN, vol_hbm.at[0, pl.ds(0, HALO)], halo.at[1], b - 1, s)
     to_sibling = remote(SIBLING, tomo_hbm, block_at(s), b, sibling)
     to_other = remote(OTHER, tomo_hbm, block_at(s), b, other)
@@ -262,17 +260,19 @@
     last_planes = tomo_hbm.at[pl.ds(block - RADIUS, RADIUS)]
     first_planes = tomo_hbm.at[pl.ds(0, RADIUS)]
     low_a = remote(LOW_A, last_planes, low_edge, b + 1, 3)
-    low_b = remote(LOW_B, last_planes, low_edge, b + 1, 1)
+    low_b = remote(LOW_B, tomo.at[pl.ds(E, RADIUS)], low_edge, b + 1, 1)
     low_relay = remote(LOW_RELAY, low_edge, low_edge, b, sibling)
     high_a = remote(HIGH_A, first_planes, high_edge, b - 1, 0)
-    high_b = remote(HIGH_B, first_planes, high_edge, b - 1, 2)
+    high_b = remote(HIGH_B, tomo.at[pl.ds(RADIUS, RADIUS)], high_edge, b - 1, 2)
     high_relay = remote(HIGH_RELAY, high_edge, high_edge, b, sibling)
-    node = remote(NODE, sub_ref, above, b - 1, s)
+    node = remote(NODE, sub_hbm, above, b - 1, s)
 
     get_own = pltpu.make_async_copy(vol_hbm.at[0], own, local.at[0])
     get_tomo = pltpu.make_async_copy(tomo_hbm, block_at(s), local.at[1])
+    get_sub = pltpu.make_async_copy(sub_hbm, mine, local.at[2])
     get_own.start()
     get_tomo.start()
+    get_sub.start()
 
     barrier = pltpu.get_barrier_semaphore()
 
@@ -288,29 +288,11 @@
     def _():
         greet(b + 1, s)
 
-        @pl.when(s == 3)
-        def _():
-            greet(b + 1, 1)
-
-        @pl.when(s == 2)
-        def _():
-            greet(b + 1, 0)
-
     @pl.when(has_below)
     def _():
         greet(b - 1, s)
 
-        @pl.when(s == 1)
-        def _():
-            greet(b - 1, 3)
-
-        @pl.when(s == 0)
-        def _():
-            greet(b - 1, 2)
-
-    from_above = jnp.where(has_above, jnp.where(s >= 2, 2, 1), 0)
-    from_below = jnp.where(has_below, jnp.where(s <= 1, 2, 1), 0)
-    pl.semaphore_wait(barrier, 2 + from_above + from_below)
+    pl.semaphore_wait(barrier, 2 + has_above.astype(jnp.int32) + has_below.astype(jnp.int32))
 
     to_other.start()
     to_sibling.start()
@@ -318,21 +300,19 @@
     @pl.when(has_above & (s == 3))
     def _():
         low_a.start()
-        low_b.start()
 
     @pl.when(has_below & (s == 0))
     def _():
         high_a.start()
-        high_b.start()
+
+    @pl.when(has_below)
+    def _():
+        node.start()
+        down.start()
 
     @pl.when(has_above)
     def _():
         up.start()
-
-    @pl.when(has_below)
-    def _():
-        down.start()
-        node.start()
 
     zeros_lo = jnp.zeros((YPAD, NXY), jnp.float32)
     zeros_hi = jnp.zeros((VROWS - YPAD - NXY, NXY), jnp.float32)
@@ -344,8 +324,10 @@
 
     lax.fori_loop(0, VPLANES, borders, 0)
     nodes[...] = jnp.zeros_like(nodes)
+    halo[0, 0] = jnp.zeros((NXY, NXY), jnp.bfloat16)
+    get_sub.wait()
     for c in range(3):
-        nodes[c : c + 1, : NODES * NODES] = sub_ref[0, c]
+        nodes[c : c + 1, : NODES * NODES] = mine[0, c]
 
     @pl.when(jnp.logical_not(has_below))
     def _():
@@ -365,8 +347,27 @@
 
     lax.fori_loop(0, E, spread_own, 0)
 
+    def filter_block(i):
+        filter_planes(band_x, band_y, tomo, grads, RADIUS + block * i, block)
+
+    write_bands(band_x, band_y)
+    get_tomo.wait()
+    filter_block(s)
+
     from_other.wait_recv()
     relay.start()
+
+    @pl.when(has_above & (s == 1))
+    def _():
+        low_b.start()
+
+    @pl.when(has_below & (s == 2))
+    def _():
+        high_b.start()
+
+    filter_block(other)
+    from_sibling.wait_recv()
+    filter_block(sibling)
 
     @pl.when(has_below & odd)
     def _():
@@ -392,32 +393,36 @@
 
         high_relay.start()
 
-    get_tomo.wait()
-    from_sibling.wait_recv()
-    from_relay.wait_recv()
-
-    @pl.when(has_below & jnp.logical_not(odd))
-    def _():
-        low_relay.wait_recv()
-
-    @pl.when(has_above & odd)
-    def _():
-        high_relay.wait_recv()
-
-    filter_planes(tomo, xf, grads)
+    write_shifts(offs, shifts)
 
     @pl.when(has_above)
     def _():
         node.wait_recv()
         for c in range(3):
             nodes[8 + c : 9 + c, : NODES * NODES] = above[0, c]
+
+    node_fields(nodes, fields)
+    from_relay.wait_recv()
+    filter_block(lax.rem(sibling + 2, 4))
+
+    @pl.when(has_below & jnp.logical_not(odd))
+    def _():
+        low_relay.wait_recv()
+
+    @pl.when(has_above & odd)
+    def _():
+        high_relay.wait_recv()
+
+    filter_planes(band_x, band_y, tomo, grads, 0, RADIUS)
+    filter_planes(band_x, band_y, tomo, grads, RADIUS + E, RADIUS)
+
+    @pl.when(has_above)
+    def _():
         down.wait_recv()
 
     @pl.when(has_below)
     def _():
         up.wait_recv()
-
-    node_fields(nodes, fields)
 
     def spread_halo(z, _):
         volf[z, YPAD : YPAD + NXY] = halo[0, z].astype(jnp.float32)
@@ -428,9 +433,11 @@
 
     def put_row(ey):
         rows = pl.ds(pl.multiple_of(ey * E, E), E)
-        return pltpu.make_async_copy(res.at[:, rows], res_hbm.at[:, rows], local.at[2 + ey])
-
-    warp_layer(offs, fields, volf, tomo, grads, lhs, win, ysum, res, lambda ey: put_row(ey).start())
+        return pltpu.make_async_copy(res.at[:, rows], res_hbm.at[:, rows], local.at[3 + ey])
+
+    warp_layer(
+        offs, shifts, fields, volf, tomo, grads, lhs, win, ysum, res, lambda ey: put_row(ey).start()
+    )
     sums[...] = node_sums(ysum)
     to_above = remote(TAIL, sums.at[pl.ds(8, 8)], tail, b + 1, s)
 
@@ -445,11 +452,17 @@
     @pl.when(has_above & (s == 3))
     def _():
         low_a.wait_send()
+
+    @pl.when(has_above & (s == 1))
+    def _():
         low_b.wait_send()
 
     @pl.when(has_below & (s == 0))
     def _():
         high_a.wait_send()
+
+    @pl.when(has_below & (s == 2))
+    def _():
         high_b.wait_send()
 
     @pl.when(has_below & odd)
@@ -493,21 +506,24 @@
     tall = E + 2 * RADIUS
     smem = pl.BlockSpec(memory_space=pltpu.SMEM)
     vmem = pl.BlockSpec(memory_space=pltpu.VMEM)
-    hbm = pl.BlockSpec(memory_space=pl.ANY)
+    hbm = pl.BlockSpec(memory_space=pltpu.HBM)
     residual, node_rhs = pl.pallas_call(
         step_kernel,
         out_shape=(
             jax.ShapeDtypeStruct((E, NXY, NXY), jnp.bfloat16),
             jax.ShapeDtypeStruct(subvoxel.shape, jnp.float32),
         ),
-        in_specs=[smem, vmem, hbm, hbm],
+        in_specs=[smem, hbm, hbm, hbm],
         out_specs=(hbm, vmem),
         scratch_shapes=[
             pltpu.VMEM((E, NXY, NXY), jnp.bfloat16),
             pltpu.VMEM((2, HALO, NXY, NXY), jnp.bfloat16),
             pltpu.VMEM((tall, NXY, NXY), jnp.bfloat16),
+            pltpu.VMEM((E, NXY, NXY), jnp.bfloat16),
             pltpu.VMEM((VPLANES, VROWS, NXY), jnp.float32),
-            pltpu.VMEM((tall, NXY, 2 * NXY), jnp.bfloat16),
+            pltpu.VMEM((NXY, 2 * NXY), jnp.bfloat16),
+            pltpu.VMEM((2 * NXY, NXY), jnp.bfloat16),
+            pltpu.VMEM((PER_ROW, PER_ROW * NXY, 2 * NXY), jnp.bfloat16),
             pltpu.VMEM((3, tall, NXY, NXY), jnp.float32),
             pltpu.VMEM((WPLANES * WIN, PER_ROW * NXY), jnp.bfloat16),
             pltpu.VMEM((2, WPLANES * WIN, NXY), jnp.float32),
@@ -515,17 +531,17 @@
             pltpu.VMEM((NODES, 16, NXY), jnp.float32),
             pltpu.VMEM((16, NXY), jnp.float32),
             pltpu.VMEM(subvoxel.shape, jnp.float32),
-            pltpu.VMEM((E, NXY, NXY), jnp.bfloat16),
+            pltpu.VMEM(subvoxel.shape, jnp.float32),
             pltpu.VMEM((16, NXY), jnp.float32),
             pltpu.VMEM((8, NXY), jnp.float32),
             pltpu.SemaphoreType.DMA((13,)),
             pltpu.SemaphoreType.DMA((13,)),
-            pltpu.SemaphoreType.DMA((2 + PER_ROW,)),
+            pltpu.SemaphoreType.DMA((3 + PER_ROW,)),
         ],
         compiler_params=pltpu.CompilerParams(
-            collective_id=0, has_side_effects=True, vmem_limit_bytes=48 << 20
+            collective_id=0, has_side_effects=True, vmem_limit_bytes=60 << 20
         ),
-    )(offsets[0], subvoxel, tomogram, deformed)
+    )(offsets.transpose(1, 0, 2), subvoxel, tomogram, deformed)
     return residual[None], node_rhs
 
 

time: 54.5 us -> 48.8 us (0.90)
  the two profiles are of different devices: /device:TPU:7 before, /device:TPU:70 now
where the time goes in v3:
time: 48.8 us; the launch traced here: 48.6 us
  Pallas kernels  45.1 us (92%)
  local copies, waits for them, and re-layouts  2.87 us (6%)
  between operations  0.65 us (1%)
    pallas_call x1, Pallas kernels, body(): pl.pallas_call(step_kernel, out_shape=(jax.ShapeDtypeStruct((E, NXY, NXY)...  45.1 us
    unnamed x4, local copies, waits for them, and re-layouts  2.87 us

profile of v3, /device:TPU:70, one launch (start us, length us, event | category | flops | bytes accessed | tf_op | source)
XLA Modules:
  0.0 48.6 jit_solution(11420031212823369340)
XLA Ops:
  0.6 45.1 %shard_map.59 = (bf16[32,128,128]{2,1,0:T(8,128)(2,1)}, f32[1,3,1,25]{3,2,1,0:T(1,128)}) custom-call(s32[3,1,16]{2,1,0:T(1,128)} %bitcast.3, f32[1,3,1,25]{3,2,1,0:T(1,128)} %sub_hbm.1, bf16[8,128,128]{2,1,0:T(8,128)(2,1)} %tomo_hbm.1, bf16[1,32,128,128]{3,2,1,0:T(8,128)(2,1)} %vol_hbm.1), custom_call_target="tpu_custom_call" | custom-call | tf_op jit(solution)/shard_map/pallas_call | solution.py:510
  45.7 0.0 copy-start
  45.7 2.3 %copy.8 = bf16[1,32,128,128]{3,2,1,0:T(8,128)(2,1)} copy(bf16[1,32,128,128]{3,2,1,0:T(8,128)(2,1)} %bitcast.2) | data formatting | bytes 2097152
  48.1 0.0 copy-done
  48.1 0.6 %copy.9 = f32[1,3,1,25]{3,2,1,0:T(1,128)} copy(f32[1,3,1,25]{3,2,1,0:T(1,128)S(1)} %copy-done) | data formatting | bytes 600
Async XLA Ops:
  45.7 2.3 %copy-start = (f32[1,3,1,25]{3,2,1,0:T(1,128)S(1)}, f32[1,3,1,25]{3,2,1,0:T(1,128)}, u32[]{:S(2)}) copy-start(f32[1,3,1,25]{3,2,1,0:T(1,128)} %get-tuple-element.9) | copy-start | bytes 904

commit v4 on v3

--- a/solution.py
+++ b/solution.py
@@ -64,6 +64,29 @@
         grads[0, start + k] = out[:NXY, :NXY]
         grads[1, start + k] = out[NXY:, :NXY]
         grads[2, start + k] = out[:NXY, NXY:]
+
+
+def filter_depth(grads):
+    strips = NXY // 16
+
+    def step(i, _):
+        z0 = i // strips * GROUP
+        rows = pl.ds(pl.multiple_of(i % strips * 16, 16), 16)
+        for c in range(3):
+            g = [grads[c, z0 + k, rows, :] for k in range(GROUP + 2 * RADIUS)]
+            for k in range(GROUP):
+                if c == 0:
+                    grad = g[k + 4] - g[k + 2]
+                    for t in (2, 3):
+                        grad = grad + (SLOPE[3 + t] / SLOPE[4]) * (g[k + 3 + t] - g[k + 3 - t])
+                else:
+                    grad = g[k + 3]
+                    for t in (1, 2, 3):
+                        grad = grad + (SMOOTH[3 + t] / SMOOTH[3]) * (g[k + 3 + t] + g[k + 3 - t])
+                grads[c, z0 + k, rows, :] = grad
+        return 0
+
+    lax.fori_loop(0, E // GROUP * strips, step, 0)
 
 
 def write_shifts(offs, shifts):
@@ -86,25 +109,31 @@
 def warp_layer(offs, shifts, fields, volf, tomo_ref, grads, lhs, win, ysum, res_ref, row_done):
     ysum[...] = jnp.zeros_like(ysum)
 
+    def gather_planes(ey, q):
+        for ex in range(PER_ROW):
+            oz = offs[0, 0, ey * PER_ROW + ex] + HALO
+            oy = offs[1, 0, ey * PER_ROW + ex] + ey * E + YPAD
+            two = []
+            for k in range(2):
+                z = jnp.minimum(2 * q + k + oz, VPLANES - 1)
+                two.append(volf[z, pl.ds(oy, WIN), :])
+            lhs[ey % 2, pl.ds(pl.multiple_of(q * 2 * WIN, 2 * WIN), 2 * WIN), ex * NXY : (ex + 1) * NXY] = (
+                jnp.concatenate(two, axis=0).astype(jnp.bfloat16)
+            )
+
+    def gather_first(q, _):
+        gather_planes(0, q)
+        return 0
+
+    lax.fori_loop(0, WPLANES // 2, gather_first, 0)
+
     def element_row(ey, _):
-        def gather_planes(q, _):
-            for ex in range(PER_ROW):
-                oz = offs[0, 0, ey * PER_ROW + ex] + HALO
-                oy = offs[1, 0, ey * PER_ROW + ex] + ey * E + YPAD
-                two = []
-                for k in range(2):
-                    z = jnp.minimum(2 * q + k + oz, VPLANES - 1)
-                    two.append(volf[z, pl.ds(oy, WIN), :])
-                lhs[pl.ds(pl.multiple_of(q * 2 * WIN, 2 * WIN), 2 * WIN), ex * NXY : (ex + 1) * NXY] = (
-                    jnp.concatenate(two, axis=0).astype(jnp.bfloat16)
-                )
-            return 0
-
-        lax.fori_loop(0, WPLANES // 2, gather_planes, 0)
+        after = jnp.minimum(ey + 1, PER_ROW - 1)
+        gather_planes(after, WPLANES // 2 - 1)
         rows = WPLANES * WIN
         for r0 in range(0, rows, 480):
             r1 = min(r0 + 480, rows)
-            out = jnp.dot(lhs[r0:r1, :], shifts[ey], preferred_element_type=jnp.float32)
+            out = jnp.dot(lhs[ey % 2, r0:r1, :], shifts[ey], preferred_element_type=jnp.float32)
             win[0, r0:r1, :] = out[:, :NXY]
             win[1, r0:r1, :] = out[:, NXY:]
 
@@ -126,6 +155,7 @@
             def planes_step(group, carry):
                 sums, prefix = list(carry[:3]), list(carry[3:])
                 z0 = group * GROUP
+                gather_planes(after, group + half * (E // GROUP))
 
                 def corner_rows(z):
                     r = pl.multiple_of(z * WIN, 8) + 16 * half
@@ -157,17 +187,8 @@
                     misfits.append(misfit)
                     lower = upper
                 for c in range(3):
-                    g = [grads[c, z0 + k, pl.ds(yrow, 16), :] for k in range(GROUP + 2 * RADIUS)]
                     for k in range(GROUP):
-                        if c == 0:
-                            grad = g[k + 4] - g[k + 2]
-                            for t in (2, 3):
-                                grad = grad + (SLOPE[3 + t] / SLOPE[4]) * (g[k + 3 + t] - g[k + 3 - t])
-                        else:
-                            grad = g[k + 3]
-                            for t in (1, 2, 3):
-                                grad = grad + (SMOOTH[3 + t] / SMOOTH[3]) * (g[k + 3 + t] + g[k + 3 - t])
-                        sums[c] = sums[c] + grad * misfits[k]
+                        sums[c] = sums[c] + grads[c, z0 + k, pl.ds(yrow, 16), :] * misfits[k]
                         prefix[c] = prefix[c] + sums[c]
                 return (*sums, *prefix)
 
@@ -220,9 +241,9 @@
 
 
 def step_kernel(
-    offs, sub_hbm, tomo_hbm, vol_hbm, res_hbm, rhs_ref,
+    offs_hbm, sub_hbm, tomo_hbm, vol_hbm, res_hbm, rhs_ref,
     own, halo, tomo, res, volf, band_x, band_y, shifts, grads, lhs, win, ysum, fields, nodes, mine, above, sums, tail,
-    send, recv, local,
+    offs, send, recv, local,
 ):
     bricks = lax.axis_size("brick")
     b = lax.axis_index("brick")
@@ -269,6 +290,8 @@
 
     get_own = pltpu.make_async_copy(vol_hbm.at[0], own, local.at[0])
     get_tomo = pltpu.make_async_copy(tomo_hbm, block_at(s), local.at[1])
+    get_offs = pltpu.make_async_copy(offs_hbm, offs, local.at[3 + PER_ROW])
+    get_offs.start()
     get_sub = pltpu.make_async_copy(sub_hbm, mine, local.at[2])
     get_own.start()
     get_tomo.start()
@@ -308,11 +331,6 @@
     @pl.when(has_below)
     def _():
         node.start()
-        down.start()
-
-    @pl.when(has_above)
-    def _():
-        up.start()
 
     zeros_lo = jnp.zeros((YPAD, NXY), jnp.float32)
     zeros_hi = jnp.zeros((VROWS - YPAD - NXY, NXY), jnp.float32)
@@ -357,6 +375,15 @@
     from_other.wait_recv()
     relay.start()
 
+    @pl.when(has_below)
+    def _():
+        down.start()
+
+    @pl.when(has_above)
+    def _():
+        up.start()
+
+
     @pl.when(has_above & (s == 1))
     def _():
         low_b.start()
@@ -393,6 +420,7 @@
 
         high_relay.start()
 
+    get_offs.wait()
     write_shifts(offs, shifts)
 
     @pl.when(has_above)
@@ -415,6 +443,7 @@
 
     filter_planes(band_x, band_y, tomo, grads, 0, RADIUS)
     filter_planes(band_x, band_y, tomo, grads, RADIUS + E, RADIUS)
+    filter_depth(grads)
 
     @pl.when(has_above)
     def _():
@@ -513,7 +542,7 @@
             jax.ShapeDtypeStruct((E, NXY, NXY), jnp.bfloat16),
             jax.ShapeDtypeStruct(subvoxel.shape, jnp.float32),
         ),
-        in_specs=[smem, hbm, hbm, hbm],
+        in_specs=[hbm, hbm, hbm, hbm],
         out_specs=(hbm, vmem),
         scratch_shapes=[
             pltpu.VMEM((E, NXY, NXY), jnp.bfloat16),
@@ -525,7 +554,7 @@
             pltpu.VMEM((2 * NXY, NXY), jnp.bfloat16),
             pltpu.VMEM((PER_ROW, PER_ROW * NXY, 2 * NXY), jnp.bfloat16),
             pltpu.VMEM((3, tall, NXY, NXY), jnp.float32),
-            pltpu.VMEM((WPLANES * WIN, PER_ROW * NXY), jnp.bfloat16),
+            pltpu.VMEM((2, WPLANES * WIN, PER_ROW * NXY), jnp.bfloat16),
             pltpu.VMEM((2, WPLANES * WIN, NXY), jnp.float32),
             pltpu.VMEM((NODES, 16, NXY), jnp.float32),
             pltpu.VMEM((NODES, 16, NXY), jnp.float32),
@@ -534,14 +563,20 @@
             pltpu.VMEM(subvoxel.shape, jnp.float32),
             pltpu.VMEM((16, NXY), jnp.float32),
             pltpu.VMEM((8, NXY), jnp.float32),
+            pltpu.SMEM((3, 1, PER_ROW * PER_ROW), jnp.int32),
             pltpu.SemaphoreType.DMA((13,)),
             pltpu.SemaphoreType.DMA((13,)),
-            pltpu.SemaphoreType.DMA((3 + PER_ROW,)),
+            pltpu.SemaphoreType.DMA((4 + PER_ROW,)),
         ],
         compiler_params=pltpu.CompilerParams(
-            collective_id=0, has_side_effects=True, vmem_limit_bytes=60 << 20
+            collective_id=0, has_side_effects=True, vmem_limit_bytes=50 << 20
         ),
-    )(offsets.transpose(1, 0, 2), subvoxel, tomogram, deformed)
+    )(
+        *[
+            pltpu.with_memory_space_constraint(x, pltpu.HBM)
+            for x in (offsets.transpose(1, 0, 2), subvoxel, tomogram, deformed)
+        ],
+    )
     return residual[None], node_rhs
 
 

time: 48.8 us -> 44.9 us (0.920)
  Pallas kernels: 45.1 us -> 42.6 us
  local copies, waits for them, and re-layouts: 2.87 us -> 1.53 us
    pallas_call x1, Pallas kernels: 45.1 us -> 42.6 us  [body(): pl.pallas_call(step_kernel, out_shape=(jax.ShapeDtypeStruct((E, NXY, NXY)...]
    unnamed x4 -> x2, local copies, waits for them, and re-layouts: 2.87 us -> 1.53 us
where the time goes in v4:
time: 44.9 us; the launch traced here: 44.8 us
  Pallas kernels  42.6 us (95%)
  local copies, waits for them, and re-layouts  1.53 us (3%)
  between operations  0.64 us (1%)
    pallas_call x1, Pallas kernels, body(): pl.pallas_call(step_kernel, out_shape=(jax.ShapeDtypeStruct((E, NXY, NXY)...  42.6 us
    unnamed x2, local copies, waits for them, and re-layouts  1.53 us

profile of v4, /device:TPU:70, one launch (start us, length us, event | category | flops | bytes accessed | tf_op | source)
XLA Modules:
  0.0 44.8 jit_solution(14055575685799428325)
XLA Ops:
  0.6 42.6 %shard_map.59 = (bf16[32,128,128]{2,1,0:T(8,128)(2,1)S(1)}, f32[1,3,1,25]{3,2,1,0:T(1,128)S(1)}) custom-call(s32[3,1,16]{2,1,0:T(1,128)} %bitcast.3, f32[1,3,1,25]{3,2,1,0:T(1,128)} %sub_hbm.1, bf16[8,128,128]{2,1,0:T(8,128)(2,1)} %tomo_hbm.1, bf16[1,32,128,128]{3,2,1,0:T(8,128)(2,1)} %vol_hbm.1), custom_call_target="tpu_custom_call" | custom-call | tf_op jit(solution)/shard_map/pallas_call | solution.py:539
  43.2 1.0 %copy.8 = bf16[1,32,128,128]{3,2,1,0:T(8,128)(2,1)} copy(bf16[1,32,128,128]{3,2,1,0:T(8,128)(2,1)S(1)} %bitcast.2) | data formatting | bytes 2097152
  44.2 0.6 %copy.9 = f32[1,3,1,25]{3,2,1,0:T(1,128)} copy(f32[1,3,1,25]{3,2,1,0:T(1,128)S(1)} %get-tuple-element.9) | data formatting | bytes 600

commit v5 on v4

--- a/solution.py
+++ b/solution.py
@@ -106,7 +106,7 @@
     lax.fori_loop(0, PER_ROW, element_row, 0)
 
 
-def warp_layer(offs, shifts, fields, volf, tomo_ref, grads, lhs, win, ysum, res_ref, row_done):
+def warp_layer(offs, shifts, fields, volf, tomo_ref, grads, lhs, win, ysum, res_ref):
     ysum[...] = jnp.zeros_like(ysum)
 
     def gather_planes(ey, q):
@@ -166,7 +166,6 @@
                         win[1, pl.ds(r + 1, 16), :],
                     )
 
-                misfits = []
                 lower = corner_rows(z0)
                 for k in range(GROUP):
                     z = z0 + k
@@ -184,12 +183,10 @@
                     ref = tomo_ref[z + RADIUS, pl.ds(yrow, 16), :].astype(jnp.float32)
                     misfit = t0 + wz * (t1 - t0) - ref
                     res_ref[z, pl.ds(yrow, 16), :] = misfit.astype(jnp.bfloat16)
-                    misfits.append(misfit)
+                    for c in range(3):
+                        sums[c] = sums[c] + grads[c, z, pl.ds(yrow, 16), :] * misfit
+                        prefix[c] = prefix[c] + sums[c]
                     lower = upper
-                for c in range(3):
-                    for k in range(GROUP):
-                        sums[c] = sums[c] + grads[c, z0 + k, pl.ds(yrow, 16), :] * misfits[k]
-                        prefix[c] = prefix[c] + sums[c]
                 return (*sums, *prefix)
 
             zero = jnp.zeros((16, NXY), jnp.float32)
@@ -203,7 +200,6 @@
                         row = jnp.sum(part * weight, axis=0, keepdims=True)
                         at = p * 8 + c
                         ysum[ey + j, at : at + 1, :] = ysum[ey + j, at : at + 1, :] + row
-        row_done(ey)
         return 0
 
     lax.fori_loop(0, PER_ROW, element_row, 0)
@@ -217,22 +213,23 @@
     return jnp.where(node < NODES, weight, 0.0)
 
 
-def node_fields(nodes, fields):
+def node_fields(nodes, fields, lanes):
     for iy in range(NODES):
+        lanes[iy] = node_lanes(iy)
         fields[iy] = lax.dot_general(
             nodes[...],
-            node_lanes(iy),
+            lanes[iy],
             (((1,), (1,)), ((), ())),
             preferred_element_type=jnp.float32,
             precision=lax.Precision.HIGHEST,
         )
 
 
-def node_sums(ysum):
+def node_sums(ysum, lanes):
     total = jnp.zeros((16, NXY), jnp.float32)
     for iy in range(NODES):
         total = total + jnp.dot(
-            ysum[iy], node_lanes(iy), preferred_element_type=jnp.float32, precision=lax.Precision.HIGHEST
+            ysum[iy], lanes[iy], preferred_element_type=jnp.float32, precision=lax.Precision.HIGHEST
         )
     return total
 
@@ -241,8 +238,8 @@
 
 
 def step_kernel(
-    offs_hbm, sub_hbm, tomo_hbm, vol_hbm, res_hbm, rhs_ref,
-    own, halo, tomo, res, volf, band_x, band_y, shifts, grads, lhs, win, ysum, fields, nodes, mine, above, sums, tail,
+    offs_hbm, sub_hbm, tomo_hbm, vol_hbm, res, rhs_ref,
+    own, halo, tomo, lanes, volf, band_x, band_y, shifts, grads, lhs, win, ysum, fields, nodes, mine, above, sums, tail,
     offs, send, recv, local,
 ):
     bricks = lax.axis_size("brick")
@@ -290,7 +287,7 @@
 
     get_own = pltpu.make_async_copy(vol_hbm.at[0], own, local.at[0])
     get_tomo = pltpu.make_async_copy(tomo_hbm, block_at(s), local.at[1])
-    get_offs = pltpu.make_async_copy(offs_hbm, offs, local.at[3 + PER_ROW])
+    get_offs = pltpu.make_async_copy(offs_hbm, offs, local.at[3])
     get_offs.start()
     get_sub = pltpu.make_async_copy(sub_hbm, mine, local.at[2])
     get_own.start()
@@ -317,16 +314,16 @@
 
     pl.semaphore_wait(barrier, 2 + has_above.astype(jnp.int32) + has_below.astype(jnp.int32))
 
+    @pl.when(has_above & (s == 3))
+    def _():
+        low_a.start()
+
+    @pl.when(has_below & (s == 0))
+    def _():
+        high_a.start()
+
     to_other.start()
     to_sibling.start()
-
-    @pl.when(has_above & (s == 3))
-    def _():
-        low_a.start()
-
-    @pl.when(has_below & (s == 0))
-    def _():
-        high_a.start()
 
     @pl.when(has_below)
     def _():
@@ -373,15 +370,16 @@
     filter_block(s)
 
     from_other.wait_recv()
+
+    @pl.when(has_below)
+    def _():
+        down.start()
+
+    @pl.when(has_above)
+    def _():
+        up.start()
+
     relay.start()
-
-    @pl.when(has_below)
-    def _():
-        down.start()
-
-    @pl.when(has_above)
-    def _():
-        up.start()
 
 
     @pl.when(has_above & (s == 1))
@@ -429,7 +427,7 @@
         for c in range(3):
             nodes[8 + c : 9 + c, : NODES * NODES] = above[0, c]
 
-    node_fields(nodes, fields)
+    node_fields(nodes, fields, lanes)
     from_relay.wait_recv()
     filter_block(lax.rem(sibling + 2, 4))
 
@@ -460,14 +458,10 @@
 
     lax.fori_loop(0, HALO, spread_halo, 0)
 
-    def put_row(ey):
-        rows = pl.ds(pl.multiple_of(ey * E, E), E)
-        return pltpu.make_async_copy(res.at[:, rows], res_hbm.at[:, rows], local.at[3 + ey])
-
     warp_layer(
-        offs, shifts, fields, volf, tomo, grads, lhs, win, ysum, res, lambda ey: put_row(ey).start()
+        offs, shifts, fields, volf, tomo, grads, lhs, win, ysum, res
     )
-    sums[...] = node_sums(ysum)
+    sums[...] = node_sums(ysum, lanes)
     to_above = remote(TAIL, sums.at[pl.ds(8, 8)], tail, b + 1, s)
 
     @pl.when(has_above)
@@ -510,9 +504,6 @@
     def _():
         down.wait_send()
         node.wait_send()
-
-    for ey in range(PER_ROW):
-        put_row(ey).wait()
 
     @pl.when(jnp.logical_not(has_below))
     def _():
@@ -543,12 +534,12 @@
             jax.ShapeDtypeStruct(subvoxel.shape, jnp.float32),
         ),
         in_specs=[hbm, hbm, hbm, hbm],
-        out_specs=(hbm, vmem),
+        out_specs=(vmem, vmem),
         scratch_shapes=[
             pltpu.VMEM((E, NXY, NXY), jnp.bfloat16),
             pltpu.VMEM((2, HALO, NXY, NXY), jnp.bfloat16),
             pltpu.VMEM((tall, NXY, NXY), jnp.bfloat16),
-            pltpu.VMEM((E, NXY, NXY), jnp.bfloat16),
+            pltpu.VMEM((NODES, NXY, NXY), jnp.float32),
             pltpu.VMEM((VPLANES, VROWS, NXY), jnp.float32),
             pltpu.VMEM((NXY, 2 * NXY), jnp.bfloat16),
             pltpu.VMEM((2 * NXY, NXY), jnp.bfloat16),
@@ -566,7 +557,7 @@
             pltpu.SMEM((3, 1, PER_ROW * PER_ROW), jnp.int32),
             pltpu.SemaphoreType.DMA((13,)),
             pltpu.SemaphoreType.DMA((13,)),
-            pltpu.SemaphoreType.DMA((4 + PER_ROW,)),
+            pltpu.SemaphoreType.DMA((4,)),
         ],
         compiler_params=pltpu.CompilerParams(
             collective_id=0, has_side_effects=True, vmem_limit_bytes=50 << 20

time: 44.9 us -> 44.7 us (level)
  no operation moved by 1% of the time
where the time goes in v5:
time: 44.7 us; the launch traced here: 44.6 us
  Pallas kernels  42.4 us (95%)
  local copies, waits for them, and re-layouts  1.53 us (3%)
  between operations  0.64 us (1%)
    pallas_call x1, Pallas kernels, body(): pl.pallas_call(step_kernel, out_shape=(jax.ShapeDtypeStruct((E, NXY, NXY)...  42.4 us
    unnamed x2, local copies, waits for them, and re-layouts  1.53 us

profile of v5, /device:TPU:70, one launch (start us, length us, event | category | flops | bytes accessed | tf_op | source)
XLA Modules:
  0.0 44.6 jit_solution(13225713266644575418)
XLA Ops:
  0.6 42.4 %shard_map.59 = (bf16[32,128,128]{2,1,0:T(8,128)(2,1)S(1)}, f32[1,3,1,25]{3,2,1,0:T(1,128)S(1)}) custom-call(s32[3,1,16]{2,1,0:T(1,128)} %bitcast.3, f32[1,3,1,25]{3,2,1,0:T(1,128)} %sub_hbm.1, bf16[8,128,128]{2,1,0:T(8,128)(2,1)} %tomo_hbm.1, bf16[1,32,128,128]{3,2,1,0:T(8,128)(2,1)} %vol_hbm.1), custom_call_target="tpu_custom_call" | custom-call | tf_op jit(solution)/shard_map/pallas_call | solution.py:530
  43.0 1.0 %copy.8 = bf16[1,32,128,128]{3,2,1,0:T(8,128)(2,1)} copy(bf16[1,32,128,128]{3,2,1,0:T(8,128)(2,1)S(1)} %bitcast.2) | data formatting | bytes 2097152
  44.0 0.6 %copy.9 = f32[1,3,1,25]{3,2,1,0:T(1,128)} copy(f32[1,3,1,25]{3,2,1,0:T(1,128)S(1)} %get-tuple-element.9) | data formatting | bytes 600

commit v6 on v5

--- a/solution.py
+++ b/solution.py
@@ -370,17 +370,16 @@
     filter_block(s)
 
     from_other.wait_recv()
-
-    @pl.when(has_below)
+    relay.start()
+
+    @pl.when(has_below & (lax.rem(b, 4) == 0))
     def _():
         down.start()
 
-    @pl.when(has_above)
+    @pl.when(has_above & (lax.rem(b, 4) == 3))
     def _():
         up.start()
 
-    relay.start()
-
 
     @pl.when(has_above & (s == 1))
     def _():
@@ -391,6 +390,15 @@
         high_b.start()
 
     filter_block(other)
+
+    @pl.when(has_below & (lax.rem(b, 4) != 0))
+    def _():
+        down.start()
+
+    @pl.when(has_above & (lax.rem(b, 4) != 3))
+    def _():
+        up.start()
+
     from_sibling.wait_recv()
     filter_block(sibling)
 

time: 44.7 us -> 44.7 us (level)
  no operation moved by 1% of the time
where the time goes in v6:
time: 44.7 us; the launch traced here: 44.6 us
  Pallas kernels  42.4 us (95%)
  local copies, waits for them, and re-layouts  1.53 us (3%)
  between operations  0.64 us (1%)
    pallas_call x1, Pallas kernels, body(): pl.pallas_call(step_kernel, out_shape=(jax.ShapeDtypeStruct((E, NXY, NXY)...  42.4 us
    unnamed x2, local copies, waits for them, and re-layouts  1.53 us

profile of v6, /device:TPU:70, one launch (start us, length us, event | category | flops | bytes accessed | tf_op | source)
XLA Modules:
  0.0 44.6 jit_solution(8427617494440130860)
XLA Ops:
  0.6 42.4 %shard_map.59 = (bf16[32,128,128]{2,1,0:T(8,128)(2,1)S(1)}, f32[1,3,1,25]{3,2,1,0:T(1,128)S(1)}) custom-call(s32[3,1,16]{2,1,0:T(1,128)} %bitcast.3, f32[1,3,1,25]{3,2,1,0:T(1,128)} %sub_hbm.1, bf16[8,128,128]{2,1,0:T(8,128)(2,1)} %tomo_hbm.1, bf16[1,32,128,128]{3,2,1,0:T(8,128)(2,1)} %vol_hbm.1), custom_call_target="tpu_custom_call" | custom-call | tf_op jit(solution)/shard_map/pallas_call | solution.py:538
  43.0 1.0 %copy.8 = bf16[1,32,128,128]{3,2,1,0:T(8,128)(2,1)} copy(bf16[1,32,128,128]{3,2,1,0:T(8,128)(2,1)S(1)} %bitcast.2) | data formatting | bytes 2097152
  44.0 0.6 %copy.9 = f32[1,3,1,25]{3,2,1,0:T(1,128)} copy(f32[1,3,1,25]{3,2,1,0:T(1,128)S(1)} %get-tuple-element.9) | data formatting | bytes 600
